TPU v7x, 256 devices: a whole 4x4x8 slice. The times are simulated.
256 devices in a mesh: energy: 8 (over x, z_hi), strip: 32 (over y, z_lo, core).
Axes of the slice: x: 4, y: 4, z: 8 (z_hi: 2, z_lo: 4; z = z_hi * 4 + z_lo), core: 2. Of those that a mesh axis runs over, the one named last changes fastest.
Arguments:
- object_field: float32 [64, 2, 2048, 384], P('energy', None, 'strip'), may hold values from -5 to 5
- probe_modes: float32 [64, 3, 2, 128, 128], P('energy'), may hold values from -2.5 to 2.5
- measured: float32 [64, 32, 5, 128, 128], P('energy', 'strip'), may hold values from 0.5 to 3
- scan_cols: int32 [32, 5], replicated, may hold values from 0 to 256, as said below
- spectra: float32 [64, 2, 8], replicated, may hold values from -4 to 4
- material_order: int32 [8], replicated, may hold values from 0 to 7, each once
Outputs:
- refined_object: float32 [64, 2, 2048, 384], P('energy', None, 'strip')
- abundance: float32 [8, 2, 32, 64, 384], P(None, None, 'strip', 'energy')
Inputs may be any that keep to these rules, and one draw needn't show every extreme that they name: `scan_cols`: row b lists the first columns of the scan positions of band b, whose top row is b * 64; they rise, neighbours differ by 32 to 96, the first is 0 and the last 256. `material_order`: each material once.
All inputs are finite; a program needn't handle non-finite values.
Results may differ from a plain program's by a relative error of at most 0.0013.
Values sent between devices are 32-bit elements; how exact they have to be, the bound alone decides.
No kernel may reach another device: no remote copies, remote signals or barrier semaphores. Data moves between devices by JAX's collectives and lax.ppermute only.
A program may use at most 64 MiB of HBM per device.

v0:
```python
import jax
import jax.numpy as jnp
import numpy as np
from jax import lax
from jax.experimental import pallas as pl
from jax.experimental.pallas import tpu as pltpu
from jax.sharding import PartitionSpec as P


PRECISE = lax.Precision.HIGHEST
LANES = 128
SUBLANES = 8
GROUP = 2
CHUNK = 4


def shifted(block, axis, distance):
    devices = range(lax.axis_size(axis))
    route = [(i - distance, i) for i in devices if i - distance in devices]
    return lax.ppermute(block, axis, route)


def dft_tables(width):
    counter = np.arange(width)
    angle = 2.0 * np.pi * (counter[:, None] * counter[None, :] % width) / width
    cosine = (np.cos(angle) / np.sqrt(width)).astype(np.float32)
    sine = (np.sin(angle) / np.sqrt(width)).astype(np.float32)
    left = np.block([[cosine, sine], [-sine, cosine]])
    right = np.block([[cosine, -sine], [sine, cosine]])
    return jnp.asarray(left).astype(jnp.bfloat16), jnp.asarray(right).astype(jnp.bfloat16)


def transform(left, right, waves):
    width = waves[0][0].shape[0]
    stacked = jnp.concatenate([jnp.concatenate(pair, axis=0) for pair in waves], axis=1)
    half = jnp.dot(left, stacked, preferred_element_type=jnp.float32).astype(jnp.bfloat16)
    rows = []
    for m in range(len(waves)):
        cols = slice(m * width, (m + 1) * width)
        rows.append(jnp.concatenate([half[:width, cols], half[width:, cols]], axis=1))
    full = jnp.dot(
        jnp.concatenate(rows, axis=0), right, preferred_element_type=jnp.float32
    )
    return [
        (full[m * width:(m + 1) * width, :width], full[m * width:(m + 1) * width, width:])
        for m in range(len(waves))
    ]


def gradient_kernel(
    cols_ref, left_ref, right_ref, top_ref, low_ref, probe_ref, measured_ref,
    own_ref, carried_ref, total,
):
    energies, modes = probe_ref.shape[:2]
    width = probe_ref.shape[-1]
    half = width // 2
    left, right = left_ref[...], right_ref[...]
    lane = lax.broadcasted_iota(jnp.int32, (width, width), 1)
    power = [
        sum(probe_ref[e, m, q] * probe_ref[e, m, q] for m in range(modes) for q in range(2))
        for e in range(energies)
    ]
    step = [
        0.5 / jnp.max(jnp.max(p, axis=0, keepdims=True), axis=1, keepdims=True) for p in power
    ]

    def window(e, part, start):
        cols = pl.ds(start, LANES)
        return jnp.concatenate([top_ref[e, part, :, cols], low_ref[e, part, :, cols]], axis=0)

    bases = [0, 0, pl.multiple_of(cols_ref[2] // LANES * LANES, LANES), LANES, 2 * LANES]
    moves = [None, cols_ref[1], cols_ref[2] - bases[2], cols_ref[3] - LANES, None]

    def patch_of(e, p):
        base, offset = bases[p], moves[p]
        if offset is None:
            return [window(e, part, base) for part in range(2)]
        back = lax.rem(LANES - offset, LANES)
        patch = []
        for part in range(2):
            here = pltpu.roll(window(e, part, base), back, 1)
            there = pltpu.roll(window(e, part, base + LANES), back, 1)
            patch.append(jnp.where(lane < LANES - offset, here, there))
        return patch

    def add(e, part, start, value):
        at = pl.ds(start, LANES)
        total[e, part, :, at] += value

    def forward(p):
        waves, patches = [], [patch_of(e, p) for e in range(energies)]
        for e in range(energies):
            real, imag = patches[e]
            for m in range(modes):
                pr, pi = probe_ref[e, m, 0], probe_ref[e, m, 1]
                waves.append((
                    (pr * real - pi * imag).astype(jnp.bfloat16),
                    (pr * imag + pi * real).astype(jnp.bfloat16),
                ))
        return patches, transform(left, right, waves)

    def correction(p, spectrum):
        corrected = []
        for e in range(energies):
            mine = spectrum[e * modes:(e + 1) * modes]
            intensity = sum(r * r + i * i for r, i in mine)
            scale = measured_ref[e, p] * lax.rsqrt(jnp.maximum(intensity, 0.25))
            flipped = -scale
            corrected += [
                ((r * scale).astype(jnp.bfloat16), (i * flipped).astype(jnp.bfloat16))
                for r, i in mine
            ]
        return corrected

    def gather(p, patches, returned):
        for e in range(energies):
            patch = patches[e]
            grads = [power[e] * patch[0], power[e] * patch[1]]
            for m in range(modes):
                pr, pi = probe_ref[e, m, 0], probe_ref[e, m, 1]
                rr, ri = returned[e * modes + m]
                grads[0] -= pr * rr - pi * ri
                grads[1] += pr * ri + pi * rr
            for part, grad in enumerate(grads):
                if p == 0:
                    total[e, part, :, :LANES] = grad
                elif moves[p] is None:
                    add(e, part, bases[p], grad)
                else:
                    moved = pltpu.roll(grad, moves[p], 1)
                    add(e, part, bases[p], jnp.where(lane >= moves[p], moved, 0.0))
                    there = jnp.where(lane < moves[p], moved, 0.0)
                    if p == 1:
                        total[e, part, :, LANES:2 * LANES] = there
                        total[e, part, :, 2 * LANES:] = jnp.zeros((width, LANES), jnp.float32)
                    else:
                        add(e, part, bases[p] + LANES, there)

    patches, spectrum = forward(0)
    for p in range(5):
        corrected = correction(p, spectrum)
        ahead = forward(p + 1) if p < 4 else None
        returned = transform(left, right, corrected)
        gather(p, patches, returned)
        if ahead:
            patches, spectrum = ahead
    for e in range(energies):
        own_ref[e] = top_ref[e] - step[e] * total[e, :, :half]
        carried_ref[e] = step[e] * total[e, :, half:]


def band_update(chunk, own_cols, left, right, top, low, probe, measured):
    _, parts, rows, cols = top.shape
    _, modes, _, width, _ = probe.shape
    positions = measured.shape[1]
    start = chunk * CHUNK // GROUP
    band = pl.BlockSpec((GROUP, parts, rows, cols), lambda e: (e, 0, 0, 0))
    table = pl.BlockSpec(left.shape, lambda e: (0, 0))
    pairs = CHUNK * positions
    return pl.pallas_call(
        gradient_kernel,
        grid=(CHUNK // GROUP,),
        in_specs=[
            pl.BlockSpec(memory_space=pltpu.SMEM),
            table,
            table,
            pl.BlockSpec((GROUP, parts, rows, cols), lambda e: (e + start, 0, 0, 0)),
            band,
            pl.BlockSpec((GROUP, modes, parts, width, width), lambda e: (e + start, 0, 0, 0, 0)),
            pl.BlockSpec((GROUP, positions, width, width), lambda e: (e + start, 0, 0, 0)),
        ],
        out_specs=[band, band],
        out_shape=[jax.ShapeDtypeStruct((CHUNK, parts, rows, cols), jnp.float32)] * 2,
        scratch_shapes=[pltpu.VMEM((GROUP, parts, width, cols), jnp.float32)],
        cost_estimate=pl.CostEstimate(
            flops=pairs * 500_000_000, bytes_accessed=pairs * 200_000, transcendentals=0
        ),
        name="band_update",
    )(own_cols, left, right, top, low, probe, measured)


def spread(matrix):
    wide = jnp.kron(matrix, jnp.eye(SUBLANES, dtype=jnp.float32))
    high = lax.reduce_precision(wide, 8, 7)
    return jnp.concatenate(
        [jnp.concatenate([part, part], axis=1) for part in (high, wide - high)], axis=0
    ).astype(jnp.bfloat16)


def times(weight, values):
    high = values.astype(jnp.bfloat16)
    low = (values - high.astype(jnp.float32)).astype(jnp.bfloat16)
    products = jnp.dot(
        weight, jnp.concatenate([high, low], axis=0), preferred_element_type=jnp.float32
    )
    rows = products.shape[0] // 2
    return products[:rows] + products[rows:]


def project_kernel(place_ref, weight_ref, *refs):
    chunks = 2
    owns, received, outs = refs[:chunks], refs[chunks:2 * chunks], refs[2 * chunks:]
    energies, parts = owns[0].shape[:2]
    slots = len(outs)
    weight = weight_ref[...]
    for d in range(slots):
        at = lax.rem(place_ref[0] + d, slots)
        values = [
            own[e, q, at, 0] - got[e, q, at, 0]
            for own, got in zip(owns, received) for e in range(energies) for q in range(parts)
        ]
        outs[d][...] = times(weight, jnp.concatenate(values, axis=0))


def project(half, place, weight, owns, received):
    slots = 4
    chunk, parts, _, columns = owns[0].shape
    shape = (chunk, parts, slots, 2, SUBLANES, columns)
    block = pl.BlockSpec(shape[:3] + (1,) + shape[4:], lambda i: (0, 0, 0, half, 0, 0))
    arrays = [a.reshape(shape) for a in (*owns, *received)]
    out = jax.ShapeDtypeStruct((weight.shape[0] // 2, columns), jnp.float32)
    return pl.pallas_call(
        project_kernel,
        grid=(1,),
        in_specs=[
            pl.BlockSpec(memory_space=pltpu.SMEM), pl.BlockSpec(weight.shape, lambda i: (0, 0))
        ] + [block] * len(arrays),
        out_specs=[pl.BlockSpec(out.shape, lambda i: (0, 0))] * slots,
        out_shape=[out] * slots,
        cost_estimate=pl.CostEstimate(flops=400_000_000, bytes_accessed=2_000_000, transcendentals=0),
        name="project",
    )(place, weight, *arrays)


def expand_kernel(place_ref, weight_ref, *refs):
    slots = 4
    pieces, refined_ref = refs[:slots], refs[-1]
    parts = refined_ref.shape[1]
    weight = weight_ref[...]
    for d, piece in enumerate(pieces):
        values = times(weight, piece[...])
        at = lax.rem(place_ref[0] + slots - d, slots)
        for j in range(values.shape[0] // SUBLANES):
            refined_ref[j // parts, j % parts, at, 0] = values[j * SUBLANES:(j + 1) * SUBLANES]


def expand(half, place, weight, pieces, shape, previous):
    smem = pl.BlockSpec(memory_space=pltpu.SMEM)
    in_specs = [smem] + [pl.BlockSpec(a.shape, lambda i: (0, 0)) for a in (weight, *pieces)]
    aliases = {}
    if previous:
        aliases = {len(in_specs): 0}
        in_specs += [pl.BlockSpec(memory_space=pl.ANY)]
    return pl.pallas_call(
        expand_kernel,
        grid=(1,),
        in_specs=in_specs,
        out_specs=pl.BlockSpec(shape[:3] + (1,) + shape[4:], lambda i: (0, 0, 0, half, 0, 0)),
        out_shape=jax.ShapeDtypeStruct(shape, jnp.float32),
        input_output_aliases=aliases,
        cost_estimate=pl.CostEstimate(flops=400_000_000, bytes_accessed=2_000_000, transcendentals=0),
        name="expand",
    )(place, weight, *pieces, *previous)


def pick_kernel(place_ref, order_ref, first_ref, second_ref, out_ref):
    second = place_ref[1] == 1
    for m in range(out_ref.shape[0]):
        for q in range(out_ref.shape[1]):
            row = (order_ref[m] * out_ref.shape[1] + q) * SUBLANES
            at = pl.ds(pl.multiple_of(row, SUBLANES), SUBLANES)
            out_ref[m, q, 0] = jnp.where(second, second_ref[at], first_ref[at])


def pick(place, order, first, second, shape):
    smem = pl.BlockSpec(memory_space=pltpu.SMEM)
    vmem = pl.BlockSpec(memory_space=pltpu.VMEM)
    return pl.pallas_call(
        pick_kernel,
        in_specs=[smem, smem, vmem, vmem],
        out_specs=vmem,
        out_shape=jax.ShapeDtypeStruct(shape, jnp.float32),
        cost_estimate=pl.CostEstimate(flops=1_000_000, bytes_accessed=600_000, transcendentals=0),
        name="pick",
    )(place, order, first, second)


def build_basis(spectra):
    spectra_real = spectra[:, 0]
    spectra_imag = spectra[:, 1]
    upper_rows = jnp.stack([spectra_real, -spectra_imag], axis=-1)
    lower_rows = jnp.stack([spectra_imag, spectra_real], axis=-1)
    stacked = jnp.stack([upper_rows, lower_rows], axis=1)
    return stacked.reshape(2 * spectra.shape[0], 2 * spectra.shape[2])


def along_x(block, distance):
    return lax.ppermute(block, "energy", [(e, (e + 2 * distance) % 8) for e in range(8)])


def along_z(block):
    return lax.ppermute(block, "energy", [(e, e ^ 1) for e in range(8)])


def on_device(object_field, probe_modes, measured, scan_cols, spectra, material_order):
    energies, parts, _, columns = object_field.shape
    materials = spectra.shape[2]
    left, right = dft_tables(probe_modes.shape[-1])
    measured = measured[:, 0]
    own_cols = lax.dynamic_index_in_dim(scan_cols, lax.axis_index("strip"), 0, keepdims=False)
    lows = [
        shifted(object_field[e:e + CHUNK], "strip", -1) for e in range(0, energies, CHUNK)
    ]
    energy = lax.axis_index("energy")
    place = jnp.stack([energy // 2, energy % 2]).astype(jnp.int32)
    basis_matrix = build_basis(spectra)
    gram_matrix = jnp.dot(basis_matrix.T, basis_matrix, precision=PRECISE)
    factor = jnp.linalg.cholesky(gram_matrix)
    basis_own = lax.dynamic_slice_in_dim(
        basis_matrix, energy * energies * parts, energies * parts, axis=0
    )
    solver_own = jax.scipy.linalg.cho_solve((factor, True), basis_own.T)
    spread_solver, spread_basis = spread(solver_own), spread(basis_own)

    owns, received = [], []
    for chunk, low in enumerate(lows):
        own, carried = band_update(
            chunk, own_cols, left, right, object_field, low, probe_modes, measured
        )
        owns.append(own)
        received.append(shifted(carried, "strip", 1))
    mine = []
    for h in range(2):
        share, *others = project(h, place, spread_solver, owns, received)
        arrived = [along_x(other, d + 1) for d, other in enumerate(others)]
        share = share + arrived[0] + arrived[1] + arrived[2]
        arrived = along_z(share)
        mine.append(share + arrived)
    abundance = pick(
        place, material_order, *mine, (materials, parts, 1, SUBLANES, columns)
    )
    refined = ()
    shape = (energies, parts, 4, 2, SUBLANES, columns)
    for h in range(2):
        near = {d: along_x(mine[h], d) for d in (1, 3)}
        far = along_x(near[1 + 2 * h], 1 + 2 * h)
        pieces = [mine[h], near[1], far, near[3]]
        refined = (expand(h, place, spread_basis, pieces, shape, refined),)
    return refined[0].reshape(object_field.shape), abundance


def solution(mesh):
    return jax.shard_map(
        on_device,
        mesh=mesh,
        in_specs=(
            P("energy", None, "strip", None),
            P("energy", None, None, None, None),
            P("energy", "strip", None, None, None),
            P(),
            P(),
            P(),
        ),
        out_specs=(P("energy", None, "strip", None), P(None, None, "strip", "energy", None)),
        check_vma=False,
    )
```

profile of v0, /device:TPU:80, one launch (start us, length us, event | category | flops | bytes accessed | tf_op | source)
XLA Modules:
  0.0 116.8 jit_solution(3450386295710892549)
XLA Ops:
  2.2 1.9 %collective-permute-start = (f32[4,2,64,384]{3,2,1,0:T(8,128)S(1)}, f32[4,2,64,384]{3,2,1,0:T(8,128)}, u32[]{:S(2)}, u32[]{:S(2)}) collective-permute-start(f32[4,2,64,384]{3,2,1,0:T(8,128)S(1)} %get-tuple-element.27), channel_id=1, source_target_pairs={{1,0},{2,1},{3,2},{4,3},{5,4},{6,5},{7,6},{8,7},{9,8},{10,9},{11,1... | collective-permute-start | bytes 2359304 | tf_op jit(solution)/shard_map/ppermute | solution.py:20
  4.1 2.1 %collective-permute-start.1 = (f32[4,2,64,384]{3,2,1,0:T(8,128)S(1)}, f32[4,2,64,384]{3,2,1,0:T(8,128)}, u32[]{:S(2)}, u32[]{:S(2)}) collective-permute-start(f32[4,2,64,384]{3,2,1,0:T(8,128)S(1)} %get-tuple-element.26), channel_id=1, source_target_pairs={{1,0},{2,1},{3,2},{4,3},{5,4},{6,5},{7,6},{8,7},{9,8},{10,9},{11,1... | collective-permute-start | bytes 2359304 | tf_op jit(solution)/shard_map/ppermute | solution.py:20
  13.6 8.5 %band_update.2 = (f32[4,2,64,384]{3,2,1,0:T(8,128)}, f32[4,2,64,384]{3,2,1,0:T(8,128)}) custom-call(s32[5]{0:T(128)} %dynamic-slice_reduce_fusion.cols_ref, bf16[256,256]{1,0:T(8,128)(2,1)} %constant.100.left_ref, bf16[256,256]{1,0:T(8,128)(2,1)} %constant.101.right_ref, f32[8,2,64,384]{3,2,1,0:T(8,128)} %top_ref.3, ...), custom_call_target="tpu_custom_call" | custom-call | flops 10000000000 | bytes 4000000 | tf_op jit(solution)/shard_map/band_update/pallas_call | solution.py:160
  22.1 4.2 %collective-permute-start.2 = (f32[4,2,64,384]{3,2,1,0:T(8,128)}, f32[4,2,64,384]{3,2,1,0:T(8,128)S(1)}, u32[]{:S(2)}, u32[]{:S(2)}) collective-permute-start(f32[4,2,64,384]{3,2,1,0:T(8,128)} %get-tuple-element.16), channel_id=1, source_target_pairs={{0,1},{1,2},{2,3},{3,4},{4,5},{5,6},{6,7},{7,8},{8,9},{9,10},{10,1... | collective-permute-start | bytes 2359304 | tf_op jit(solution)/shard_map/ppermute | solution.py:20
  26.3 8.6 %band_update.3 = (f32[4,2,64,384]{3,2,1,0:T(8,128)}, f32[4,2,64,384]{3,2,1,0:T(8,128)}) custom-call(s32[5]{0:T(128)} %dynamic-slice_reduce_fusion.cols_ref, bf16[256,256]{1,0:T(8,128)(2,1)} %constant.100.left_ref, bf16[256,256]{1,0:T(8,128)(2,1)} %constant.101.right_ref, f32[8,2,64,384]{3,2,1,0:T(8,128)} %top_ref.3, ...), custom_call_target="tpu_custom_call" | custom-call | flops 10000000000 | bytes 4000000 | tf_op jit(solution)/shard_map/band_update/pallas_call | solution.py:160
  34.9 2.0 %collective-permute-start.3 = (f32[4,2,64,384]{3,2,1,0:T(8,128)}, f32[4,2,64,384]{3,2,1,0:T(8,128)}, u32[]{:S(2)}, u32[]{:S(2)}) collective-permute-start(f32[4,2,64,384]{3,2,1,0:T(8,128)} %get-tuple-element.17), channel_id=1, source_target_pairs={{0,1},{1,2},{2,3},{3,4},{4,5},{5,6},{6,7},{7,8},{8,9},{9,10},{10,1... | collective-permute-start | bytes 2359304 | tf_op jit(solution)/shard_map/ppermute | solution.py:20
  38.9 9.6 %collective-permute-done.3 = f32[4,2,64,384]{3,2,1,0:T(8,128)} collective-permute-done((f32[4,2,64,384]{3,2,1,0:T(8,128)}, f32[4,2,64,384]{3,2,1,0:T(8,128)}, u32[]{:S(2)}, u32[]{:S(2)}) %collective-permute-start.3) | collective-permute-done | bytes 786464 | tf_op jit(solution)/shard_map/ppermute | solution.py:20
  48.5 2.5 %project.2 = (f32[128,384]{1,0:T(8,128)}, f32[128,384]{1,0:T(8,128)}, f32[128,384]{1,0:T(8,128)}, f32[128,384]{1,0:T(8,128)}) custom-call(s32[2]{0:T(128)} %pad_add_fusion.place_ref, bf16[256,256]{1,0:T(8,128)(2,1)} %maximum_maximum_fusion.1.weight_ref, f32[4,2,4,2,8,384]{5,4,3,2,1,0:T(8,128)} %bitcast.42, f32[4,2,4,2,8,384]{5,4,3,2,1,0:T(8,128)} %bitcast.46, ...), custom_call_target="tpu_custom_call" | custom-call | flops 400000000 | bytes 2000000 | tf_op jit(solution)/shard_map/project/pallas_call | solution.py:222
  51.0 2.8 %collective-permute-start.6 = (f32[128,384]{1,0:T(8,128)}, f32[128,384]{1,0:T(8,128)S(1)}, u32[]{:S(2)}, u32[]{:S(2)}) collective-permute-start(f32[128,384]{1,0:T(8,128)} %get-tuple-element.21), channel_id=1, source_target_pairs={{0,192},{32,224},{64,0},{96,32},{128,64},{160,96},{192,128},{224,1... | collective-permute-start | bytes 589832 | tf_op jit(solution)/shard_map/ppermute | solution.py:298
  55.4 2.5 %project.3 = (f32[128,384]{1,0:T(8,128)}, f32[128,384]{1,0:T(8,128)}, f32[128,384]{1,0:T(8,128)}, f32[128,384]{1,0:T(8,128)}) custom-call(s32[2]{0:T(128)} %pad_add_fusion.place_ref, bf16[256,256]{1,0:T(8,128)(2,1)} %maximum_maximum_fusion.1.weight_ref, f32[4,2,4,2,8,384]{5,4,3,2,1,0:T(8,128)} %bitcast.43, f32[4,2,4,2,8,384]{5,4,3,2,1,0:T(8,128)} %bitcast.47, ...), custom_call_target="tpu_custom_call" | custom-call | flops 400000000 | bytes 2000000 | tf_op jit(solution)/shard_map/project/pallas_call | solution.py:222
  58.0 2.3 %collective-permute-start.13 = (f32[128,384]{1,0:T(8,128)}, f32[128,384]{1,0:T(8,128)S(1)}, u32[]{:S(2)}, u32[]{:S(2)}) collective-permute-start(f32[128,384]{1,0:T(8,128)} %get-tuple-element.25), channel_id=1, source_target_pairs={{0,192},{32,224},{64,0},{96,32},{128,64},{160,96},{192,128},{224,1... | collective-permute-start | bytes 589832 | tf_op jit(solution)/shard_map/ppermute | solution.py:298
  60.3 1.5 %collective-permute-start.12 = (f32[128,384]{1,0:T(8,128)}, f32[128,384]{1,0:T(8,128)S(1)}, u32[]{:S(2)}, u32[]{:S(2)}) collective-permute-start(f32[128,384]{1,0:T(8,128)} %get-tuple-element.24), channel_id=1, source_target_pairs={{0,128},{32,160},{64,192},{96,224},{128,0},{160,32},{192,64},{224,... | collective-permute-start | bytes 589832 | tf_op jit(solution)/shard_map/ppermute | solution.py:298
  62.9 5.0 %collective-permute-done.4 = f32[128,384]{1,0:T(8,128)S(1)} collective-permute-done((f32[128,384]{1,0:T(8,128)}, f32[128,384]{1,0:T(8,128)S(1)}, u32[]{:S(2)}, u32[]{:S(2)}) %collective-permute-start.4) | collective-permute-done | bytes 196640 | tf_op jit(solution)/shard_map/ppermute | solution.py:298
  67.9 4.6 %collective-permute-start.7 = (f32[128,384]{1,0:T(8,128)S(1)}, f32[128,384]{1,0:T(8,128)S(1)}, u32[]{:S(2)}, u32[]{:S(2)}) collective-permute-start(f32[128,384]{1,0:T(8,128)S(1)} %add_add_fusion.1), channel_id=1, source_target_pairs={{0,32},{32,0},{64,96},{96,64},{128,160},{160,128},{192,224},{224,1... | collective-permute-start | bytes 589832 | tf_op jit(solution)/shard_map/ppermute | solution.py:302
  72.5 3.2 %collective-permute-done.11 = f32[128,384]{1,0:T(8,128)S(1)} collective-permute-done((f32[128,384]{1,0:T(8,128)}, f32[128,384]{1,0:T(8,128)S(1)}, u32[]{:S(2)}, u32[]{:S(2)}) %collective-permute-start.11) | collective-permute-done | bytes 196640 | tf_op jit(solution)/shard_map/ppermute | solution.py:298
  76.7 5.2 %collective-permute-start.14 = (f32[128,384]{1,0:T(8,128)S(1)}, f32[128,384]{1,0:T(8,128)S(1)}, u32[]{:S(2)}, u32[]{:S(2)}) collective-permute-start(f32[128,384]{1,0:T(8,128)S(1)} %add_add_fusion), channel_id=1, source_target_pairs={{0,32},{32,0},{64,96},{96,64},{128,160},{160,128},{192,224},{224,1... | collective-permute-start | bytes 589832 | tf_op jit(solution)/shard_map/ppermute | solution.py:302
  82.6 10.4 %collective-permute-done.14 = f32[128,384]{1,0:T(8,128)S(1)} collective-permute-done((f32[128,384]{1,0:T(8,128)S(1)}, f32[128,384]{1,0:T(8,128)S(1)}, u32[]{:S(2)}, u32[]{:S(2)}) %collective-permute-start.14) | collective-permute-done | bytes 196640 | tf_op jit(solution)/shard_map/ppermute | solution.py:302
  95.1 1.9 %collective-permute-start.17 = (f32[128,384]{1,0:T(8,128)S(1)}, f32[128,384]{1,0:T(8,128)S(1)}, u32[]{:S(2)}, u32[]{:S(2)}) collective-permute-start(f32[128,384]{1,0:T(8,128)S(1)} %add.62.refs_0_.first_ref), channel_id=1, source_target_pairs={{0,192},{32,224},{64,0},{96,32},{128,64},{160,96},{192,128},{224,1... | collective-permute-start | bytes 589832 | tf_op jit(solution)/shard_map/ppermute | solution.py:298
  97.0 1.9 %collective-permute-start.10 = (f32[128,384]{1,0:T(8,128)S(1)}, f32[128,384]{1,0:T(8,128)S(1)}, u32[]{:S(2)}, u32[]{:S(2)}) collective-permute-start(f32[128,384]{1,0:T(8,128)S(1)} %collective-permute-done.9.refs_3_), channel_id=1, source_target_pairs={{0,192},{32,224},{64,0},{96,32},{128,64},{160,96},{192,128},{224,1... | collective-permute-start | bytes 589832 | tf_op jit(solution)/shard_map/ppermute | solution.py:298
  98.9 3.1 %collective-permute-done.15.refs_1_ = f32[128,384]{1,0:T(8,128)S(1)} collective-permute-done((f32[128,384]{1,0:T(8,128)S(1)}, f32[128,384]{1,0:T(8,128)S(1)}, u32[]{:S(2)}, u32[]{:S(2)}) %collective-permute-start.15) | collective-permute-done | bytes 196640 | tf_op jit(solution)/shard_map/ppermute | solution.py:298
  102.8 1.7 %pick.1 = f32[8,2,1,8,384]{4,3,2,1,0:T(8,128)} custom-call(s32[2]{0:T(128)} %pad_add_fusion.place_ref, s32[8]{0:T(128)} %order_ref.1, f32[128,384]{1,0:T(8,128)} %copy-done.3, f32[128,384]{1,0:T(8,128)} %copy-done.2), custom_call_target="tpu_custom_call" | custom-call | flops 1000000 | bytes 600000 | tf_op jit(solution)/shard_map/pick/pallas_call | solution.py:278
  104.6 5.0 %collective-permute-done.16.refs_2_ = f32[128,384]{1,0:T(8,128)S(1)} collective-permute-done((f32[128,384]{1,0:T(8,128)S(1)}, f32[128,384]{1,0:T(8,128)S(1)}, u32[]{:S(2)}, u32[]{:S(2)}) %collective-permute-start.16) | collective-permute-done | bytes 196640 | tf_op jit(solution)/shard_map/ppermute | solution.py:298
  110.3 2.6 %expand.2.refs_4_ = f32[8,2,4,2,8,384]{5,4,3,2,1,0:T(8,128)} custom-call(s32[2]{0:T(128)} %pad_add_fusion.place_ref, bf16[256,256]{1,0:T(8,128)(2,1)} %maximum_maximum_fusion.weight_ref, f32[128,384]{1,0:T(8,128)} %copy-done.3, f32[128,384]{1,0:T(8,128)} %copy-done.8, f32[128,384]{1,0:T(8,128)} %copy-done.10, f32[128,384]{1,0:T(8,128)} %copy-done.9), custom_call_target="tpu_custom_call" | custom-call | flops 400000000 | bytes 2000000 | tf_op jit(solution)/shard_map/expand/pallas_call | solution.py:254
  114.2 2.6 %expand.3 = f32[8,2,4,2,8,384]{5,4,3,2,1,0:T(8,128)} custom-call(s32[2]{0:T(128)} %pad_add_fusion.place_ref, bf16[256,256]{1,0:T(8,128)(2,1)} %maximum_maximum_fusion.weight_ref, f32[128,384]{1,0:T(8,128)} %copy-done.2, f32[128,384]{1,0:T(8,128)} %copy-done.5, f32[128,384]{1,0:T(8,128)} %copy-done.6, ...), custom_call_target="tpu_custom_call", output_to_operand_aliasing={{}: (6, {})} | custom-call | flops 400000000 | bytes 2000000 | tf_op jit(solution)/shard_map/expand/pallas_call | solution.py:254
  (76 shorter events, 20.1 us)
Async XLA Ops:
  0.6 10.4 %copy-start = (s32[32,5]{0,1:T(8,128)S(1)}, s32[32,5]{0,1:T(8,128)}, u32[]{:S(2)}) copy-start(s32[32,5]{0,1:T(8,128)} %param.11) | copy-start | bytes 1924
  2.2 11.4 %collective-permute-start = (f32[4,2,64,384]{3,2,1,0:T(8,128)S(1)}, f32[4,2,64,384]{3,2,1,0:T(8,128)}, u32[]{:S(2)}, u32[]{:S(2)}) collective-permute-start(f32[4,2,64,384]{3,2,1,0:T(8,128)S(1)} %get-tuple-element.27), channel_id=1, source_target_pairs={{1,0},{2,1},{3,2},{4,3},{5,4},{6,5},{7,6},{8,7},{9,8},{10,9},{11,1... | collective-permute-start | bytes 2359304 | tf_op jit(solution)/shard_map/ppermute | solution.py:20
  4.1 22.2 %collective-permute-start.1 = (f32[4,2,64,384]{3,2,1,0:T(8,128)S(1)}, f32[4,2,64,384]{3,2,1,0:T(8,128)}, u32[]{:S(2)}, u32[]{:S(2)}) collective-permute-start(f32[4,2,64,384]{3,2,1,0:T(8,128)S(1)} %get-tuple-element.26), channel_id=1, source_target_pairs={{1,0},{2,1},{3,2},{4,3},{5,4},{6,5},{7,6},{8,7},{9,8},{10,9},{11,1... | collective-permute-start | bytes 2359304 | tf_op jit(solution)/shard_map/ppermute | solution.py:20
  22.1 16.9 %collective-permute-start.2 = (f32[4,2,64,384]{3,2,1,0:T(8,128)}, f32[4,2,64,384]{3,2,1,0:T(8,128)S(1)}, u32[]{:S(2)}, u32[]{:S(2)}) collective-permute-start(f32[4,2,64,384]{3,2,1,0:T(8,128)} %get-tuple-element.16), channel_id=1, source_target_pairs={{0,1},{1,2},{2,3},{3,4},{4,5},{5,6},{6,7},{7,8},{8,9},{9,10},{10,1... | collective-permute-start | bytes 2359304 | tf_op jit(solution)/shard_map/ppermute | solution.py:20
  34.9 13.6 %collective-permute-start.3 = (f32[4,2,64,384]{3,2,1,0:T(8,128)}, f32[4,2,64,384]{3,2,1,0:T(8,128)}, u32[]{:S(2)}, u32[]{:S(2)}) collective-permute-start(f32[4,2,64,384]{3,2,1,0:T(8,128)} %get-tuple-element.17), channel_id=1, source_target_pairs={{0,1},{1,2},{2,3},{3,4},{4,5},{5,6},{6,7},{7,8},{8,9},{9,10},{10,1... | collective-permute-start | bytes 2359304 | tf_op jit(solution)/shard_map/ppermute | solution.py:20
  38.9 9.6 %copy-start.1 = (f32[4,2,64,384]{3,2,1,0:T(8,128)}, f32[4,2,64,384]{3,2,1,0:T(8,128)S(1)}, u32[]{:S(2)}) copy-start(f32[4,2,64,384]{3,2,1,0:T(8,128)S(1)} %collective-permute-done.2) | copy-start | bytes 2359300
  51.0 11.0 %collective-permute-start.6 = (f32[128,384]{1,0:T(8,128)}, f32[128,384]{1,0:T(8,128)S(1)}, u32[]{:S(2)}, u32[]{:S(2)}) collective-permute-start(f32[128,384]{1,0:T(8,128)} %get-tuple-element.21), channel_id=1, source_target_pairs={{0,192},{32,224},{64,0},{96,32},{128,64},{160,96},{192,128},{224,1... | collective-permute-start | bytes 589832 | tf_op jit(solution)/shard_map/ppermute | solution.py:298
  53.8 9.1 %collective-permute-start.5 = (f32[128,384]{1,0:T(8,128)}, f32[128,384]{1,0:T(8,128)S(1)}, u32[]{:S(2)}, u32[]{:S(2)}) collective-permute-start(f32[128,384]{1,0:T(8,128)} %get-tuple-element.20), channel_id=1, source_target_pairs={{0,128},{32,160},{64,192},{96,224},{128,0},{160,32},{192,64},{224,... | collective-permute-start | bytes 589832 | tf_op jit(solution)/shard_map/ppermute | solution.py:298
  54.6 13.3 %copy-start.7 = (f32[128,384]{1,0:T(8,128)S(1)}, f32[128,384]{1,0:T(8,128)}, u32[]{:S(2)}) copy-start(f32[128,384]{1,0:T(8,128)} %get-tuple-element.18) | copy-start | bytes 589828
  54.6 13.3 %collective-permute-start.4 = (f32[128,384]{1,0:T(8,128)}, f32[128,384]{1,0:T(8,128)S(1)}, u32[]{:S(2)}, u32[]{:S(2)}) collective-permute-start(f32[128,384]{1,0:T(8,128)} %get-tuple-element.19), channel_id=1, source_target_pairs={{0,64},{32,96},{64,128},{96,160},{128,192},{160,224},{192,0},{224,... | collective-permute-start | bytes 589832 | tf_op jit(solution)/shard_map/ppermute | solution.py:298
  58.0 14.5 %collective-permute-start.13 = (f32[128,384]{1,0:T(8,128)}, f32[128,384]{1,0:T(8,128)S(1)}, u32[]{:S(2)}, u32[]{:S(2)}) collective-permute-start(f32[128,384]{1,0:T(8,128)} %get-tuple-element.25), channel_id=1, source_target_pairs={{0,192},{32,224},{64,0},{96,32},{128,64},{160,96},{192,128},{224,1... | collective-permute-start | bytes 589832 | tf_op jit(solution)/shard_map/ppermute | solution.py:298
  60.3 12.2 %collective-permute-start.12 = (f32[128,384]{1,0:T(8,128)}, f32[128,384]{1,0:T(8,128)S(1)}, u32[]{:S(2)}, u32[]{:S(2)}) collective-permute-start(f32[128,384]{1,0:T(8,128)} %get-tuple-element.24), channel_id=1, source_target_pairs={{0,128},{32,160},{64,192},{96,224},{128,0},{160,32},{192,64},{224,... | collective-permute-start | bytes 589832 | tf_op jit(solution)/shard_map/ppermute | solution.py:298
  62.0 13.7 %collective-permute-start.11 = (f32[128,384]{1,0:T(8,128)}, f32[128,384]{1,0:T(8,128)S(1)}, u32[]{:S(2)}, u32[]{:S(2)}) collective-permute-start(f32[128,384]{1,0:T(8,128)} %get-tuple-element.23), channel_id=1, source_target_pairs={{0,64},{32,96},{64,128},{96,160},{128,192},{160,224},{192,0},{224,... | collective-permute-start | bytes 589832 | tf_op jit(solution)/shard_map/ppermute | solution.py:298
  67.9 14.0 %collective-permute-start.7 = (f32[128,384]{1,0:T(8,128)S(1)}, f32[128,384]{1,0:T(8,128)S(1)}, u32[]{:S(2)}, u32[]{:S(2)}) collective-permute-start(f32[128,384]{1,0:T(8,128)S(1)} %add_add_fusion.1), channel_id=1, source_target_pairs={{0,32},{32,0},{64,96},{96,64},{128,160},{160,128},{192,224},{224,1... | collective-permute-start | bytes 589832 | tf_op jit(solution)/shard_map/ppermute | solution.py:302
  76.7 16.3 %collective-permute-start.14 = (f32[128,384]{1,0:T(8,128)S(1)}, f32[128,384]{1,0:T(8,128)S(1)}, u32[]{:S(2)}, u32[]{:S(2)}) collective-permute-start(f32[128,384]{1,0:T(8,128)S(1)} %add_add_fusion), channel_id=1, source_target_pairs={{0,32},{32,0},{64,96},{96,64},{128,160},{160,128},{192,224},{224,1... | collective-permute-start | bytes 589832 | tf_op jit(solution)/shard_map/ppermute | solution.py:302
  81.9 20.9 %copy-start.2 = (f32[128,384]{1,0:T(8,128)}, f32[128,384]{1,0:T(8,128)S(1)}, u32[]{:S(2)}) copy-start(f32[128,384]{1,0:T(8,128)S(1)} %add.58.refs_0_.second_ref) | copy-start | bytes 589828
  82.0 15.0 %collective-permute-start.9 = (f32[128,384]{1,0:T(8,128)S(1)}, f32[128,384]{1,0:T(8,128)S(1)}, u32[]{:S(2)}, u32[]{:S(2)}) collective-permute-start(f32[128,384]{1,0:T(8,128)S(1)} %add.58.refs_0_.second_ref), channel_id=1, source_target_pairs={{0,192},{32,224},{64,0},{96,32},{128,64},{160,96},{192,128},{224,1... | collective-permute-start | bytes 589832 | tf_op jit(solution)/shard_map/ppermute | solution.py:298
  93.0 9.8 %copy-start.3 = (f32[128,384]{1,0:T(8,128)}, f32[128,384]{1,0:T(8,128)S(1)}, u32[]{:S(2)}) copy-start(f32[128,384]{1,0:T(8,128)S(1)} %add.62.refs_0_.first_ref) | copy-start | bytes 589828
  93.0 9.1 %collective-permute-start.15 = (f32[128,384]{1,0:T(8,128)S(1)}, f32[128,384]{1,0:T(8,128)S(1)}, u32[]{:S(2)}, u32[]{:S(2)}) collective-permute-start(f32[128,384]{1,0:T(8,128)S(1)} %add.62.refs_0_.first_ref), channel_id=1, source_target_pairs={{0,64},{32,96},{64,128},{96,160},{128,192},{160,224},{192,0},{224,... | collective-permute-start | bytes 589832 | tf_op jit(solution)/shard_map/ppermute | solution.py:298
  93.6 19.2 %collective-permute-start.8 = (f32[128,384]{1,0:T(8,128)S(1)}, f32[128,384]{1,0:T(8,128)S(1)}, u32[]{:S(2)}, u32[]{:S(2)}) collective-permute-start(f32[128,384]{1,0:T(8,128)S(1)} %add.58.refs_0_.second_ref), channel_id=1, source_target_pairs={{0,64},{32,96},{64,128},{96,160},{128,192},{160,224},{192,0},{224,... | collective-permute-start | bytes 589832 | tf_op jit(solution)/shard_map/ppermute | solution.py:298
  95.1 9.5 %collective-permute-start.17 = (f32[128,384]{1,0:T(8,128)S(1)}, f32[128,384]{1,0:T(8,128)S(1)}, u32[]{:S(2)}, u32[]{:S(2)}) collective-permute-start(f32[128,384]{1,0:T(8,128)S(1)} %add.62.refs_0_.first_ref), channel_id=1, source_target_pairs={{0,192},{32,224},{64,0},{96,32},{128,64},{160,96},{192,128},{224,1... | collective-permute-start | bytes 589832 | tf_op jit(solution)/shard_map/ppermute | solution.py:298
  97.0 15.9 %copy-start.4 = (f32[128,384]{1,0:T(8,128)}, f32[128,384]{1,0:T(8,128)S(1)}, u32[]{:S(2)}) copy-start(f32[128,384]{1,0:T(8,128)S(1)} %collective-permute-done.9.refs_3_) | copy-start | bytes 589828
  97.0 15.9 %collective-permute-start.10 = (f32[128,384]{1,0:T(8,128)S(1)}, f32[128,384]{1,0:T(8,128)S(1)}, u32[]{:S(2)}, u32[]{:S(2)}) collective-permute-start(f32[128,384]{1,0:T(8,128)S(1)} %collective-permute-done.9.refs_3_), channel_id=1, source_target_pairs={{0,192},{32,224},{64,0},{96,32},{128,64},{160,96},{192,128},{224,1... | collective-permute-start | bytes 589832 | tf_op jit(solution)/shard_map/ppermute | solution.py:298
  102.1 7.5 %collective-permute-start.16 = (f32[128,384]{1,0:T(8,128)S(1)}, f32[128,384]{1,0:T(8,128)S(1)}, u32[]{:S(2)}, u32[]{:S(2)}) collective-permute-start(f32[128,384]{1,0:T(8,128)S(1)} %collective-permute-done.15.refs_1_), channel_id=1, source_target_pairs={{0,64},{32,96},{64,128},{96,160},{128,192},{160,224},{192,0},{224,... | collective-permute-start | bytes 589832 | tf_op jit(solution)/shard_map/ppermute | solution.py:298
  (6 other events, 20.2 us)
where the time goes:
time: 117 us
  waiting for transfers between devices  38.8 us (33%)
  starting transfers between devices  34.4 us (29%)
  Pallas kernels  29 us (25%)
  other arithmetic  7.29 us (6%)
  local copies, waits for them, and re-layouts  6 us (5%)
    ppermute x12, waiting for transfers between devices, along_x(): lax.ppermute(block, 'energy', [(e, (e + 2 * distance) % 8) for e in range...  17.4 us
    pallas_call x2, Pallas kernels, band_update(): pl.pallas_call(gradient_kernel, grid=(CHUNK // GROUP,), in_specs=[pl.Bloc...  17 us
    ppermute x12, starting transfers between devices, along_x(): lax.ppermute(block, 'energy', [(e, (e + 2 * distance) % 8) for e in range...  14.4 us
    ppermute x4, waiting for transfers between devices, shifted(): return lax.ppermute(block, axis, route)  11 us
    ppermute x2, waiting for transfers between devices, along_z(): return lax.ppermute(block, 'energy', [(e, e ^ 1) for e in range(8)])  10.4 us
    ppermute x4, starting transfers between devices, shifted(): return lax.ppermute(block, axis, route)  10.2 us
    ppermute x2, starting transfers between devices, along_z(): return lax.ppermute(block, 'energy', [(e, e ^ 1) for e in range(8)])  9.81 us
    pallas_call x2, Pallas kernels, expand(): pl.pallas_call(expand_kernel, grid=(1,), in_specs=in_specs, out_specs=pl....  5.13 us
  transfers between devices with their start and end apart: 18, of which 9 were waited for; matrix products, arithmetic and copies ran while one was open for 9% of the time, Pallas kernels for 20%

commit v1 on v0

--- a/solution.py
+++ b/solution.py
@@ -1,3 +1,5 @@
+import functools
+
 import jax
 import jax.numpy as jnp
 import numpy as np
@@ -197,68 +199,108 @@
     return products[:rows] + products[rows:]
 
 
-def project_kernel(place_ref, weight_ref, *refs):
-    chunks = 2
-    owns, received, outs = refs[:chunks], refs[chunks:2 * chunks], refs[2 * chunks:]
-    energies, parts = owns[0].shape[:2]
-    slots = len(outs)
+def project_kernel(half, place_ref, weight_ref, *refs):
+    chunks, slots = 2, 4
+    sources, outs = refs[:2 * chunks], refs[2 * chunks:2 * chunks + slots]
+    taken, results, arrivals, departures = refs[2 * chunks + slots:]
     weight = weight_ref[...]
+    loads = []
     for d in range(slots):
         at = lax.rem(place_ref[0] + d, slots)
+        loads.append([
+            pltpu.make_async_copy(a.at[:, :, at, half], taken.at[d, i], arrivals.at[d, i])
+            for i, a in enumerate(sources)
+        ])
+        for load in loads[d]:
+            load.start()
+    stores = []
+    for d in range(slots):
+        for load in loads[d]:
+            load.wait()
         values = [
-            own[e, q, at, 0] - got[e, q, at, 0]
-            for own, got in zip(owns, received) for e in range(energies) for q in range(parts)
+            taken[d, i, e, q] - taken[d, chunks + i, e, q]
+            for i in range(chunks)
+            for e in range(taken.shape[2]) for q in range(taken.shape[3])
         ]
-        outs[d][...] = times(weight, jnp.concatenate(values, axis=0))
+        results[d] = times(weight, jnp.concatenate(values, axis=0))
+        stores.append(pltpu.make_async_copy(results.at[d], outs[d], departures.at[d]))
+        stores[d].start()
+    for store in stores:
+        store.wait()
 
 
 def project(half, place, weight, owns, received):
     slots = 4
     chunk, parts, _, columns = owns[0].shape
     shape = (chunk, parts, slots, 2, SUBLANES, columns)
-    block = pl.BlockSpec(shape[:3] + (1,) + shape[4:], lambda i: (0, 0, 0, half, 0, 0))
     arrays = [a.reshape(shape) for a in (*owns, *received)]
     out = jax.ShapeDtypeStruct((weight.shape[0] // 2, columns), jnp.float32)
     return pl.pallas_call(
-        project_kernel,
-        grid=(1,),
+        functools.partial(project_kernel, half),
         in_specs=[
-            pl.BlockSpec(memory_space=pltpu.SMEM), pl.BlockSpec(weight.shape, lambda i: (0, 0))
-        ] + [block] * len(arrays),
-        out_specs=[pl.BlockSpec(out.shape, lambda i: (0, 0))] * slots,
+            pl.BlockSpec(memory_space=pltpu.SMEM), pl.BlockSpec(memory_space=pltpu.VMEM)
+        ] + [pl.BlockSpec(memory_space=pl.ANY)] * len(arrays),
+        out_specs=[pl.BlockSpec(memory_space=pl.ANY)] * slots,
         out_shape=[out] * slots,
+        scratch_shapes=[
+            pltpu.VMEM((slots, len(arrays), chunk, parts, SUBLANES, columns), jnp.float32),
+            pltpu.VMEM((slots,) + out.shape, jnp.float32),
+            pltpu.SemaphoreType.DMA((slots, len(arrays))),
+            pltpu.SemaphoreType.DMA((slots,)),
+        ],
         cost_estimate=pl.CostEstimate(flops=400_000_000, bytes_accessed=2_000_000, transcendentals=0),
+        compiler_params=pltpu.CompilerParams(vmem_limit_bytes=67_000_000),
         name="project",
     )(place, weight, *arrays)
 
 
-def expand_kernel(place_ref, weight_ref, *refs):
+def expand_kernel(half, previous, place_ref, weight_ref, *refs):
     slots = 4
-    pieces, refined_ref = refs[:slots], refs[-1]
+    pieces = refs[:slots]
+    refined_ref, taken, results, arrivals, departures = refs[slots + previous:]
     parts = refined_ref.shape[1]
     weight = weight_ref[...]
-    for d, piece in enumerate(pieces):
-        values = times(weight, piece[...])
+    loads = [
+        pltpu.make_async_copy(piece, taken.at[d], arrivals.at[d]) for d, piece in enumerate(pieces)
+    ]
+    for load in loads:
+        load.start()
+    stores = []
+    for d in range(slots):
+        loads[d].wait()
+        values = times(weight, taken[d])
+        for j in range(values.shape[0] // SUBLANES):
+            results[d, j // parts, j % parts] = values[j * SUBLANES:(j + 1) * SUBLANES]
         at = lax.rem(place_ref[0] + slots - d, slots)
-        for j in range(values.shape[0] // SUBLANES):
-            refined_ref[j // parts, j % parts, at, 0] = values[j * SUBLANES:(j + 1) * SUBLANES]
+        stores.append(
+            pltpu.make_async_copy(
+                results.at[d], refined_ref.at[:, :, at, half], departures.at[d]
+            )
+        )
+        stores[d].start()
+    for store in stores:
+        store.wait()
 
 
 def expand(half, place, weight, pieces, shape, previous):
-    smem = pl.BlockSpec(memory_space=pltpu.SMEM)
-    in_specs = [smem] + [pl.BlockSpec(a.shape, lambda i: (0, 0)) for a in (weight, *pieces)]
-    aliases = {}
-    if previous:
-        aliases = {len(in_specs): 0}
-        in_specs += [pl.BlockSpec(memory_space=pl.ANY)]
+    slots = len(pieces)
+    anywhere = pl.BlockSpec(memory_space=pl.ANY)
+    in_specs = [pl.BlockSpec(memory_space=pltpu.SMEM), pl.BlockSpec(memory_space=pltpu.VMEM)]
+    in_specs += [anywhere] * (slots + len(previous))
     return pl.pallas_call(
-        expand_kernel,
-        grid=(1,),
+        functools.partial(expand_kernel, half, len(previous)),
         in_specs=in_specs,
-        out_specs=pl.BlockSpec(shape[:3] + (1,) + shape[4:], lambda i: (0, 0, 0, half, 0, 0)),
+        out_specs=anywhere,
         out_shape=jax.ShapeDtypeStruct(shape, jnp.float32),
-        input_output_aliases=aliases,
+        scratch_shapes=[
+            pltpu.VMEM((slots,) + pieces[0].shape, jnp.float32),
+            pltpu.VMEM((slots,) + shape[:2] + shape[4:], jnp.float32),
+            pltpu.SemaphoreType.DMA((slots,)),
+            pltpu.SemaphoreType.DMA((slots,)),
+        ],
+        input_output_aliases={2 + slots: 0} if previous else {},
         cost_estimate=pl.CostEstimate(flops=400_000_000, bytes_accessed=2_000_000, transcendentals=0),
+        compiler_params=pltpu.CompilerParams(vmem_limit_bytes=67_000_000),
         name="expand",
     )(place, weight, *pieces, *previous)
 
@@ -342,9 +384,7 @@
     refined = ()
     shape = (energies, parts, 4, 2, SUBLANES, columns)
     for h in range(2):
-        near = {d: along_x(mine[h], d) for d in (1, 3)}
-        far = along_x(near[1 + 2 * h], 1 + 2 * h)
-        pieces = [mine[h], near[1], far, near[3]]
+        pieces = [mine[h]] + [along_x(mine[h], d) for d in (1, 2, 3)]
         refined = (expand(h, place, spread_basis, pieces, shape, refined),)
     return refined[0].reshape(object_field.shape), abundance
 

time: 117 us -> 125 us (1.068)
  Pallas kernels: 29 us -> 33.3 us
  other arithmetic: 7.29 us -> 10.1 us
    pallas_call x4, Pallas kernels: 10.2 us -> 14.5 us  [the longest x2 7.52 us: project(): pl.pallas_call(functools.partial(project_kernel, half), in_specs=[pl.Bloc...]
  transfers between devices with their start and end apart: 18 -> 18, of which waited for: 9 -> 7; matrix products, arithmetic and copies ran while one was open for 9% -> 10% of each run, Pallas kernels for 20% -> 21%
where the time goes in v1:
time: 125 us; the launch traced here: 124 us
  waiting for transfers between devices  38.3 us (31%)
  starting transfers between devices  35.5 us (28%)
  Pallas kernels  33.3 us (27%)
  other arithmetic  10.1 us (8%)
  local copies, waits for them, and re-layouts  5.51 us (4%)
    ppermute x12, waiting for transfers between devices, along_x(): lax.ppermute(block, 'energy', [(e, (e + 2 * distance) % 8) for e in range...  17.5 us
    pallas_call x2, Pallas kernels, band_update(): pl.pallas_call(gradient_kernel, grid=(CHUNK // GROUP,), in_specs=[pl.Bloc...  17.1 us
    ppermute x12, starting transfers between devices, along_x(): lax.ppermute(block, 'energy', [(e, (e + 2 * distance) % 8) for e in range...  15.6 us
    ppermute x2, waiting for transfers between devices, along_z(): return lax.ppermute(block, 'energy', [(e, e ^ 1) for e in range(8)])  10.7 us
    ppermute x4, starting transfers between devices, shifted(): return lax.ppermute(block, axis, route)  10.1 us
    ppermute x4, waiting for transfers between devices, shifted(): return lax.ppermute(block, axis, route)  10.1 us
    ppermute x2, starting transfers between devices, along_z(): return lax.ppermute(block, 'energy', [(e, e ^ 1) for e in range(8)])  9.83 us
    pallas_call x2, Pallas kernels, project(): pl.pallas_call(functools.partial(project_kernel, half), in_specs=[pl.Bloc...  7.52 us
  transfers between devices with their start and end apart: 18, of which 7 were waited for; matrix products, arithmetic and copies ran while one was open for 10% of the time, Pallas kernels for 21%

profile of v1, /device:TPU:80, one launch (start us, length us, event | category | flops | bytes accessed | tf_op | source)
XLA Modules:
  0.0 124.3 jit_solution(4706862726026498043)
XLA Ops:
  2.2 1.9 %collective-permute-start = (f32[4,2,64,384]{3,2,1,0:T(8,128)S(1)}, f32[4,2,64,384]{3,2,1,0:T(8,128)}, u32[]{:S(2)}, u32[]{:S(2)}) collective-permute-start(f32[4,2,64,384]{3,2,1,0:T(8,128)S(1)} %get-tuple-element.27), channel_id=1, source_target_pairs={{1,0},{2,1},{3,2},{4,3},{5,4},{6,5},{7,6},{8,7},{9,8},{10,9},{11,1... | collective-permute-start | bytes 2359304 | tf_op jit(solution)/shard_map/ppermute | solution.py:22
  4.1 2.1 %collective-permute-start.1 = (f32[4,2,64,384]{3,2,1,0:T(8,128)S(1)}, f32[4,2,64,384]{3,2,1,0:T(8,128)S(1)}, u32[]{:S(2)}, u32[]{:S(2)}) collective-permute-start(f32[4,2,64,384]{3,2,1,0:T(8,128)S(1)} %get-tuple-element.26), channel_id=1, source_target_pairs={{1,0},{2,1},{3,2},{4,3},{5,4},{6,5},{7,6},{8,7},{9,8},{10,9},{11,1... | collective-permute-start | bytes 2359304 | tf_op jit(solution)/shard_map/ppermute | solution.py:22
  13.6 8.5 %band_update.2 = (f32[4,2,64,384]{3,2,1,0:T(8,128)}, f32[4,2,64,384]{3,2,1,0:T(8,128)}) custom-call(s32[5]{0:T(128)} %dynamic-slice_reduce_fusion.cols_ref, bf16[256,256]{1,0:T(8,128)(2,1)} %constant.100.left_ref, bf16[256,256]{1,0:T(8,128)(2,1)} %constant.101.right_ref, f32[8,2,64,384]{3,2,1,0:T(8,128)} %top_ref.3, ...), custom_call_target="tpu_custom_call" | custom-call | flops 10000000000 | bytes 4000000 | tf_op jit(solution)/shard_map/band_update/pallas_call | solution.py:162
  22.1 4.2 %collective-permute-start.2 = (f32[4,2,64,384]{3,2,1,0:T(8,128)}, f32[4,2,64,384]{3,2,1,0:T(8,128)}, u32[]{:S(2)}, u32[]{:S(2)}) collective-permute-start(f32[4,2,64,384]{3,2,1,0:T(8,128)} %get-tuple-element.16), channel_id=1, source_target_pairs={{0,1},{1,2},{2,3},{3,4},{4,5},{5,6},{6,7},{7,8},{8,9},{9,10},{10,1... | collective-permute-start | bytes 2359304 | tf_op jit(solution)/shard_map/ppermute | solution.py:22
  27.2 8.6 %band_update.3 = (f32[4,2,64,384]{3,2,1,0:T(8,128)}, f32[4,2,64,384]{3,2,1,0:T(8,128)}) custom-call(s32[5]{0:T(128)} %dynamic-slice_reduce_fusion.cols_ref, bf16[256,256]{1,0:T(8,128)(2,1)} %constant.100.left_ref, bf16[256,256]{1,0:T(8,128)(2,1)} %constant.101.right_ref, f32[8,2,64,384]{3,2,1,0:T(8,128)} %top_ref.3, f32[4,2,64,384]{3,2,1,0:T(8,128)} %copy-done.6, ...), custom_call_target="tpu_custom_call" | custom-call | flops 10000000000 | bytes 4000000 | tf_op jit(solution)/shard_map/band_update/pallas_call | solution.py:162
  35.7 1.9 %collective-permute-start.3 = (f32[4,2,64,384]{3,2,1,0:T(8,128)}, f32[4,2,64,384]{3,2,1,0:T(8,128)}, u32[]{:S(2)}, u32[]{:S(2)}) collective-permute-start(f32[4,2,64,384]{3,2,1,0:T(8,128)} %get-tuple-element.17), channel_id=1, source_target_pairs={{0,1},{1,2},{2,3},{3,4},{4,5},{5,6},{6,7},{7,8},{8,9},{9,10},{10,1... | collective-permute-start | bytes 2359304 | tf_op jit(solution)/shard_map/ppermute | solution.py:22
  40.7 8.7 %collective-permute-done.3 = f32[4,2,64,384]{3,2,1,0:T(8,128)} collective-permute-done((f32[4,2,64,384]{3,2,1,0:T(8,128)}, f32[4,2,64,384]{3,2,1,0:T(8,128)}, u32[]{:S(2)}, u32[]{:S(2)}) %collective-permute-start.3) | collective-permute-done | bytes 786464 | tf_op jit(solution)/shard_map/ppermute | solution.py:22
  49.4 3.7 %project.3 = (f32[128,384]{1,0:T(8,128)}, f32[128,384]{1,0:T(8,128)}, f32[128,384]{1,0:T(8,128)}, f32[128,384]{1,0:T(8,128)}) custom-call(s32[2]{0:T(128)} %pad_add_fusion.place_ref, bf16[256,256]{1,0:T(8,128)(2,1)} %maximum_maximum_fusion.1.weight_ref, f32[4,2,4,2,8,384]{5,4,3,2,1,0:T(8,128)} %bitcast.42, f32[4,2,4,2,8,384]{5,4,3,2,1,0:T(8,128)} %bitcast.44, ...), custom_call_target="tpu_custom_call" | custom-call | flops 400000000 | bytes 2000000 | tf_op jit(solution)/shard_map/project/pallas_call | solution.py:238
  53.1 2.8 %collective-permute-start.13 = (f32[128,384]{1,0:T(8,128)}, f32[128,384]{1,0:T(8,128)}, u32[]{:S(2)}, u32[]{:S(2)}) collective-permute-start(f32[128,384]{1,0:T(8,128)} %get-tuple-element.25), channel_id=1, source_target_pairs={{0,192},{32,224},{64,0},{96,32},{128,64},{160,96},{192,128},{224,1... | collective-permute-start | bytes 589832 | tf_op jit(solution)/shard_map/ppermute | solution.py:340
  57.6 3.8 %project.2 = (f32[128,384]{1,0:T(8,128)}, f32[128,384]{1,0:T(8,128)}, f32[128,384]{1,0:T(8,128)}, f32[128,384]{1,0:T(8,128)}) custom-call(s32[2]{0:T(128)} %pad_add_fusion.place_ref, bf16[256,256]{1,0:T(8,128)(2,1)} %maximum_maximum_fusion.1.weight_ref, f32[4,2,4,2,8,384]{5,4,3,2,1,0:T(8,128)} %bitcast.43, f32[4,2,4,2,8,384]{5,4,3,2,1,0:T(8,128)} %bitcast.45, ...), custom_call_target="tpu_custom_call" | custom-call | flops 400000000 | bytes 2000000 | tf_op jit(solution)/shard_map/project/pallas_call | solution.py:238
  61.4 2.6 %collective-permute-start.6 = (f32[128,384]{1,0:T(8,128)}, f32[128,384]{1,0:T(8,128)S(1)}, u32[]{:S(2)}, u32[]{:S(2)}) collective-permute-start(f32[128,384]{1,0:T(8,128)} %get-tuple-element.21), channel_id=1, source_target_pairs={{0,192},{32,224},{64,0},{96,32},{128,64},{160,96},{192,128},{224,1... | collective-permute-start | bytes 589832 | tf_op jit(solution)/shard_map/ppermute | solution.py:340
  64.0 1.5 %collective-permute-start.5 = (f32[128,384]{1,0:T(8,128)}, f32[128,384]{1,0:T(8,128)S(1)}, u32[]{:S(2)}, u32[]{:S(2)}) collective-permute-start(f32[128,384]{1,0:T(8,128)} %get-tuple-element.20), channel_id=1, source_target_pairs={{0,128},{32,160},{64,192},{96,224},{128,0},{160,32},{192,64},{224,... | collective-permute-start | bytes 589832 | tf_op jit(solution)/shard_map/ppermute | solution.py:340
  65.6 4.5 %collective-permute-done.11 = f32[128,384]{1,0:T(8,128)} collective-permute-done((f32[128,384]{1,0:T(8,128)}, f32[128,384]{1,0:T(8,128)}, u32[]{:S(2)}, u32[]{:S(2)}) %collective-permute-start.11) | collective-permute-done | bytes 196640 | tf_op jit(solution)/shard_map/ppermute | solution.py:340
  71.3 4.8 %collective-permute-start.14 = (f32[128,384]{1,0:T(8,128)S(1)}, f32[128,384]{1,0:T(8,128)S(1)}, u32[]{:S(2)}, u32[]{:S(2)}) collective-permute-start(f32[128,384]{1,0:T(8,128)S(1)} %add_add_fusion), channel_id=1, source_target_pairs={{0,32},{32,0},{64,96},{96,64},{128,160},{160,128},{192,224},{224,1... | collective-permute-start | bytes 589832 | tf_op jit(solution)/shard_map/ppermute | solution.py:344
  76.1 2.0 %collective-permute-done.4 = f32[128,384]{1,0:T(8,128)S(1)} collective-permute-done((f32[128,384]{1,0:T(8,128)}, f32[128,384]{1,0:T(8,128)S(1)}, u32[]{:S(2)}, u32[]{:S(2)}) %collective-permute-start.4) | collective-permute-done | bytes 196640 | tf_op jit(solution)/shard_map/ppermute | solution.py:340
  79.1 5.0 %collective-permute-start.7 = (f32[128,384]{1,0:T(8,128)S(1)}, f32[128,384]{1,0:T(8,128)S(1)}, u32[]{:S(2)}, u32[]{:S(2)}) collective-permute-start(f32[128,384]{1,0:T(8,128)S(1)} %add_add_fusion.1), channel_id=1, source_target_pairs={{0,32},{32,0},{64,96},{96,64},{128,160},{160,128},{192,224},{224,1... | collective-permute-start | bytes 589832 | tf_op jit(solution)/shard_map/ppermute | solution.py:344
  84.8 10.7 %collective-permute-done.7 = f32[128,384]{1,0:T(8,128)S(1)} collective-permute-done((f32[128,384]{1,0:T(8,128)S(1)}, f32[128,384]{1,0:T(8,128)S(1)}, u32[]{:S(2)}, u32[]{:S(2)}) %collective-permute-start.7) | collective-permute-done | bytes 196640 | tf_op jit(solution)/shard_map/ppermute | solution.py:344
  96.2 2.1 %collective-permute-start.9 = (f32[128,384]{1,0:T(8,128)}, f32[128,384]{1,0:T(8,128)}, u32[]{:S(2)}, u32[]{:S(2)}) collective-permute-start(f32[128,384]{1,0:T(8,128)} %add.58.refs_0_.second_ref), channel_id=1, source_target_pairs={{0,128},{32,160},{64,192},{96,224},{128,0},{160,32},{192,64},{224,... | collective-permute-start | bytes 589832 | tf_op jit(solution)/shard_map/ppermute | solution.py:340
  99.4 2.9 %collective-permute-start.16 = (f32[128,384]{1,0:T(8,128)S(1)}, f32[128,384]{1,0:T(8,128)S(1)}, u32[]{:S(2)}, u32[]{:S(2)}) collective-permute-start(f32[128,384]{1,0:T(8,128)S(1)} %add.62.refs_0_.first_ref), channel_id=1, source_target_pairs={{0,128},{32,160},{64,192},{96,224},{128,0},{160,32},{192,64},{224,... | collective-permute-start | bytes 589832 | tf_op jit(solution)/shard_map/ppermute | solution.py:340
  103.7 1.7 %pick.1 = f32[8,2,1,8,384]{4,3,2,1,0:T(8,128)} custom-call(s32[2]{0:T(128)} %pad_add_fusion.place_ref, s32[8]{0:T(128)} %order_ref.1, f32[128,384]{1,0:T(8,128)} %copy-done.2, f32[128,384]{1,0:T(8,128)} %add.58.refs_0_.second_ref), custom_call_target="tpu_custom_call" | custom-call | flops 1000000 | bytes 600000 | tf_op jit(solution)/shard_map/pick/pallas_call | solution.py:320
  105.4 6.1 %collective-permute-done.16.refs_2_ = f32[128,384]{1,0:T(8,128)S(1)} collective-permute-done((f32[128,384]{1,0:T(8,128)S(1)}, f32[128,384]{1,0:T(8,128)S(1)}, u32[]{:S(2)}, u32[]{:S(2)}) %collective-permute-start.16) | collective-permute-done | bytes 196640 | tf_op jit(solution)/shard_map/ppermute | solution.py:340
  112.2 4.9 %collective-permute-done.17.refs_3_ = f32[128,384]{1,0:T(8,128)} collective-permute-done((f32[128,384]{1,0:T(8,128)S(1)}, f32[128,384]{1,0:T(8,128)}, u32[]{:S(2)}, u32[]{:S(2)}) %collective-permute-start.17) | collective-permute-done | bytes 196640 | tf_op jit(solution)/shard_map/ppermute | solution.py:340
  117.1 3.5 %expand.2.refs_4_ = f32[8,2,4,2,8,384]{5,4,3,2,1,0:T(8,128)} custom-call(s32[2]{0:T(128)} %pad_add_fusion.place_ref, bf16[256,256]{1,0:T(8,128)(2,1)} %maximum_maximum_fusion.weight_ref, f32[128,384]{1,0:T(8,128)} %copy-done.2, f32[128,384]{1,0:T(8,128)} %copy-done.3, f32[128,384]{1,0:T(8,128)} %copy-done.4, f32[128,384]{1,0:T(8,128)} %collective-permute-done.17.refs_3_), custom_call_target="tpu_custom_call" | custom-call | flops 400000000 | bytes 2000000 | tf_op jit(solution)/shard_map/expand/pallas_call | solution.py:290
  120.7 3.5 %expand.3 = f32[8,2,4,2,8,384]{5,4,3,2,1,0:T(8,128)} custom-call(s32[2]{0:T(128)} %pad_add_fusion.place_ref, bf16[256,256]{1,0:T(8,128)(2,1)} %maximum_maximum_fusion.weight_ref, f32[128,384]{1,0:T(8,128)} %add.58.refs_0_.second_ref, f32[128,384]{1,0:T(8,128)} %collective-permute-done.8.refs_1_, ...), custom_call_target="tpu_custom_call", output_to_operand_aliasing={{}: (6, {})} | custom-call | flops 400000000 | bytes 2000000 | tf_op jit(solution)/shard_map/expand/pallas_call | solution.py:290
  (66 shorter events, 21.1 us)
Async XLA Ops:
  0.6 10.4 %copy-start = (s32[32,5]{0,1:T(8,128)S(1)}, s32[32,5]{0,1:T(8,128)}, u32[]{:S(2)}) copy-start(s32[32,5]{0,1:T(8,128)} %param.11) | copy-start | bytes 1924
  0.6 5.6 %copy-start.5 = (f32[64,2,8]{0,2,1:T(8,128)S(1)}, f32[64,2,8]{0,2,1:T(8,128)}, u32[]{:S(2)}) copy-start(f32[64,2,8]{0,2,1:T(8,128)} %param.12) | copy-start | bytes 12292
  2.2 11.4 %collective-permute-start = (f32[4,2,64,384]{3,2,1,0:T(8,128)S(1)}, f32[4,2,64,384]{3,2,1,0:T(8,128)}, u32[]{:S(2)}, u32[]{:S(2)}) collective-permute-start(f32[4,2,64,384]{3,2,1,0:T(8,128)S(1)} %get-tuple-element.27), channel_id=1, source_target_pairs={{1,0},{2,1},{3,2},{4,3},{5,4},{6,5},{7,6},{8,7},{9,8},{10,9},{11,1... | collective-permute-start | bytes 2359304 | tf_op jit(solution)/shard_map/ppermute | solution.py:22
  4.1 22.2 %collective-permute-start.1 = (f32[4,2,64,384]{3,2,1,0:T(8,128)S(1)}, f32[4,2,64,384]{3,2,1,0:T(8,128)S(1)}, u32[]{:S(2)}, u32[]{:S(2)}) collective-permute-start(f32[4,2,64,384]{3,2,1,0:T(8,128)S(1)} %get-tuple-element.26), channel_id=1, source_target_pairs={{1,0},{2,1},{3,2},{4,3},{5,4},{6,5},{7,6},{8,7},{9,8},{10,9},{11,1... | collective-permute-start | bytes 2359304 | tf_op jit(solution)/shard_map/ppermute | solution.py:22
  22.1 18.6 %collective-permute-start.2 = (f32[4,2,64,384]{3,2,1,0:T(8,128)}, f32[4,2,64,384]{3,2,1,0:T(8,128)}, u32[]{:S(2)}, u32[]{:S(2)}) collective-permute-start(f32[4,2,64,384]{3,2,1,0:T(8,128)} %get-tuple-element.16), channel_id=1, source_target_pairs={{0,1},{1,2},{2,3},{3,4},{4,5},{5,6},{6,7},{7,8},{8,9},{9,10},{10,1... | collective-permute-start | bytes 2359304 | tf_op jit(solution)/shard_map/ppermute | solution.py:22
  26.3 0.9 copy-start.6
  35.7 13.6 %collective-permute-start.3 = (f32[4,2,64,384]{3,2,1,0:T(8,128)}, f32[4,2,64,384]{3,2,1,0:T(8,128)}, u32[]{:S(2)}, u32[]{:S(2)}) collective-permute-start(f32[4,2,64,384]{3,2,1,0:T(8,128)} %get-tuple-element.17), channel_id=1, source_target_pairs={{0,1},{1,2},{2,3},{3,4},{4,5},{5,6},{6,7},{7,8},{8,9},{9,10},{10,1... | collective-permute-start | bytes 2359304 | tf_op jit(solution)/shard_map/ppermute | solution.py:22
  53.1 12.4 %collective-permute-start.13 = (f32[128,384]{1,0:T(8,128)}, f32[128,384]{1,0:T(8,128)}, u32[]{:S(2)}, u32[]{:S(2)}) collective-permute-start(f32[128,384]{1,0:T(8,128)} %get-tuple-element.25), channel_id=1, source_target_pairs={{0,192},{32,224},{64,0},{96,32},{128,64},{160,96},{192,128},{224,1... | collective-permute-start | bytes 589832 | tf_op jit(solution)/shard_map/ppermute | solution.py:340
  55.9 9.6 %collective-permute-start.12 = (f32[128,384]{1,0:T(8,128)}, f32[128,384]{1,0:T(8,128)}, u32[]{:S(2)}, u32[]{:S(2)}) collective-permute-start(f32[128,384]{1,0:T(8,128)} %get-tuple-element.24), channel_id=1, source_target_pairs={{0,128},{32,160},{64,192},{96,224},{128,0},{160,32},{192,64},{224,... | collective-permute-start | bytes 589832 | tf_op jit(solution)/shard_map/ppermute | solution.py:340
  56.7 13.3 %collective-permute-start.11 = (f32[128,384]{1,0:T(8,128)}, f32[128,384]{1,0:T(8,128)}, u32[]{:S(2)}, u32[]{:S(2)}) collective-permute-start(f32[128,384]{1,0:T(8,128)} %get-tuple-element.23), channel_id=1, source_target_pairs={{0,64},{32,96},{64,128},{96,160},{128,192},{160,224},{192,0},{224,... | collective-permute-start | bytes 589832 | tf_op jit(solution)/shard_map/ppermute | solution.py:340
  61.4 22.8 %copy-start.1 = (f32[16,8,16,8]{3,2,1,0:T(8,128)S(1)}, f32[16,8,16,8]{3,2,1,0:T(8,128)}, u32[]{:S(2)}) copy-start(f32[16,8,16,8]{3,2,1,0:T(8,128)} %get-tuple-element.35) | copy-start | bytes 196612
  61.4 14.7 %collective-permute-start.6 = (f32[128,384]{1,0:T(8,128)}, f32[128,384]{1,0:T(8,128)S(1)}, u32[]{:S(2)}, u32[]{:S(2)}) collective-permute-start(f32[128,384]{1,0:T(8,128)} %get-tuple-element.21), channel_id=1, source_target_pairs={{0,192},{32,224},{64,0},{96,32},{128,64},{160,96},{192,128},{224,1... | collective-permute-start | bytes 589832 | tf_op jit(solution)/shard_map/ppermute | solution.py:340
  64.0 12.1 %collective-permute-start.5 = (f32[128,384]{1,0:T(8,128)}, f32[128,384]{1,0:T(8,128)S(1)}, u32[]{:S(2)}, u32[]{:S(2)}) collective-permute-start(f32[128,384]{1,0:T(8,128)} %get-tuple-element.20), channel_id=1, source_target_pairs={{0,128},{32,160},{64,192},{96,224},{128,0},{160,32},{192,64},{224,... | collective-permute-start | bytes 589832 | tf_op jit(solution)/shard_map/ppermute | solution.py:340
  65.6 12.5 %collective-permute-start.4 = (f32[128,384]{1,0:T(8,128)}, f32[128,384]{1,0:T(8,128)S(1)}, u32[]{:S(2)}, u32[]{:S(2)}) collective-permute-start(f32[128,384]{1,0:T(8,128)} %get-tuple-element.19), channel_id=1, source_target_pairs={{0,64},{32,96},{64,128},{96,160},{128,192},{160,224},{192,0},{224,... | collective-permute-start | bytes 589832 | tf_op jit(solution)/shard_map/ppermute | solution.py:340
  71.3 12.8 %collective-permute-start.14 = (f32[128,384]{1,0:T(8,128)S(1)}, f32[128,384]{1,0:T(8,128)S(1)}, u32[]{:S(2)}, u32[]{:S(2)}) collective-permute-start(f32[128,384]{1,0:T(8,128)S(1)} %add_add_fusion), channel_id=1, source_target_pairs={{0,32},{32,0},{64,96},{96,64},{128,160},{160,128},{192,224},{224,1... | collective-permute-start | bytes 589832 | tf_op jit(solution)/shard_map/ppermute | solution.py:344
  79.1 16.4 %collective-permute-start.7 = (f32[128,384]{1,0:T(8,128)S(1)}, f32[128,384]{1,0:T(8,128)S(1)}, u32[]{:S(2)}, u32[]{:S(2)}) collective-permute-start(f32[128,384]{1,0:T(8,128)S(1)} %add_add_fusion.1), channel_id=1, source_target_pairs={{0,32},{32,0},{64,96},{96,64},{128,160},{160,128},{192,224},{224,1... | collective-permute-start | bytes 589832 | tf_op jit(solution)/shard_map/ppermute | solution.py:344
  84.1 19.6 %copy-start.2 = (f32[128,384]{1,0:T(8,128)}, f32[128,384]{1,0:T(8,128)S(1)}, u32[]{:S(2)}) copy-start(f32[128,384]{1,0:T(8,128)S(1)} %add.62.refs_0_.first_ref) | copy-start | bytes 589828
  84.2 18.2 %collective-permute-start.15 = (f32[128,384]{1,0:T(8,128)S(1)}, f32[128,384]{1,0:T(8,128)S(1)}, u32[]{:S(2)}, u32[]{:S(2)}) collective-permute-start(f32[128,384]{1,0:T(8,128)S(1)} %add.62.refs_0_.first_ref), channel_id=1, source_target_pairs={{0,64},{32,96},{64,128},{96,160},{128,192},{160,224},{192,0},{224,... | collective-permute-start | bytes 589832 | tf_op jit(solution)/shard_map/ppermute | solution.py:340
  96.2 24.5 %collective-permute-start.8 = (f32[128,384]{1,0:T(8,128)}, f32[128,384]{1,0:T(8,128)}, u32[]{:S(2)}, u32[]{:S(2)}) collective-permute-start(f32[128,384]{1,0:T(8,128)} %add.58.refs_0_.second_ref), channel_id=1, source_target_pairs={{0,64},{32,96},{64,128},{96,160},{128,192},{160,224},{192,0},{224,... | collective-permute-start | bytes 589832 | tf_op jit(solution)/shard_map/ppermute | solution.py:340
  96.2 24.5 %collective-permute-start.9 = (f32[128,384]{1,0:T(8,128)}, f32[128,384]{1,0:T(8,128)}, u32[]{:S(2)}, u32[]{:S(2)}) collective-permute-start(f32[128,384]{1,0:T(8,128)} %add.58.refs_0_.second_ref), channel_id=1, source_target_pairs={{0,128},{32,160},{64,192},{96,224},{128,0},{160,32},{192,64},{224,... | collective-permute-start | bytes 589832 | tf_op jit(solution)/shard_map/ppermute | solution.py:340
  98.3 22.3 %collective-permute-start.10 = (f32[128,384]{1,0:T(8,128)}, f32[128,384]{1,0:T(8,128)}, u32[]{:S(2)}, u32[]{:S(2)}) collective-permute-start(f32[128,384]{1,0:T(8,128)} %add.58.refs_0_.second_ref), channel_id=1, source_target_pairs={{0,192},{32,224},{64,0},{96,32},{128,64},{160,96},{192,128},{224,1... | collective-permute-start | bytes 589832 | tf_op jit(solution)/shard_map/ppermute | solution.py:340
  99.4 12.1 %collective-permute-start.16 = (f32[128,384]{1,0:T(8,128)S(1)}, f32[128,384]{1,0:T(8,128)S(1)}, u32[]{:S(2)}, u32[]{:S(2)}) collective-permute-start(f32[128,384]{1,0:T(8,128)S(1)} %add.62.refs_0_.first_ref), channel_id=1, source_target_pairs={{0,128},{32,160},{64,192},{96,224},{128,0},{160,32},{192,64},{224,... | collective-permute-start | bytes 589832 | tf_op jit(solution)/shard_map/ppermute | solution.py:340
  102.4 9.2 %copy-start.3 = (f32[128,384]{1,0:T(8,128)}, f32[128,384]{1,0:T(8,128)S(1)}, u32[]{:S(2)}) copy-start(f32[128,384]{1,0:T(8,128)S(1)} %collective-permute-done.15.refs_1_) | copy-start | bytes 589828
  102.4 14.8 %collective-permute-start.17 = (f32[128,384]{1,0:T(8,128)S(1)}, f32[128,384]{1,0:T(8,128)}, u32[]{:S(2)}, u32[]{:S(2)}) collective-permute-start(f32[128,384]{1,0:T(8,128)S(1)} %add.62.refs_0_.first_ref), channel_id=1, source_target_pairs={{0,192},{32,224},{64,0},{96,32},{128,64},{160,96},{192,128},{224,1... | collective-permute-start | bytes 589832 | tf_op jit(solution)/shard_map/ppermute | solution.py:340
  (1 other events, 0.7 us)

commit v2 on v0

--- a/solution.py
+++ b/solution.py
@@ -49,11 +49,12 @@
 
 def gradient_kernel(
     cols_ref, left_ref, right_ref, top_ref, low_ref, probe_ref, measured_ref,
-    own_ref, carried_ref, total,
+    own_ref, *refs,
 ):
     energies, modes = probe_ref.shape[:2]
     width = probe_ref.shape[-1]
     half = width // 2
+    *carried_refs, total = refs
     left, right = left_ref[...], right_ref[...]
     lane = lax.broadcasted_iota(jnp.int32, (width, width), 1)
     power = [
@@ -146,7 +147,12 @@
             patches, spectrum = ahead
     for e in range(energies):
         own_ref[e] = top_ref[e] - step[e] * total[e, :, :half]
-        carried_ref[e] = step[e] * total[e, :, half:]
+        if len(carried_refs) == 1:
+            carried_refs[0][e] = step[e] * total[e, :, half:]
+        else:
+            for group in range(half // SUBLANES):
+                at = slice(half + group * SUBLANES, half + (group + 1) * SUBLANES)
+                carried_refs[group % 2][e, :, group // 2, 0] = step[e] * total[e, :, at]
 
 
 def band_update(chunk, own_cols, left, right, top, low, probe, measured):
@@ -157,6 +163,12 @@
     band = pl.BlockSpec((GROUP, parts, rows, cols), lambda e: (e, 0, 0, 0))
     table = pl.BlockSpec(left.shape, lambda e: (0, 0))
     pairs = CHUNK * positions
+    if chunk == 0:
+        carried, carried_shapes = band, [(CHUNK, parts, rows, cols)]
+    else:
+        tail = (parts, rows // (2 * SUBLANES), 1, SUBLANES, cols)
+        carried = pl.BlockSpec((GROUP,) + tail, lambda e: (e, 0, 0, 0, 0, 0))
+        carried_shapes = [(CHUNK,) + tail] * 2
     return pl.pallas_call(
         gradient_kernel,
         grid=(CHUNK // GROUP,),
@@ -169,8 +181,11 @@
             pl.BlockSpec((GROUP, modes, parts, width, width), lambda e: (e + start, 0, 0, 0, 0)),
             pl.BlockSpec((GROUP, positions, width, width), lambda e: (e + start, 0, 0, 0)),
         ],
-        out_specs=[band, band],
-        out_shape=[jax.ShapeDtypeStruct((CHUNK, parts, rows, cols), jnp.float32)] * 2,
+        out_specs=[band] + [carried] * len(carried_shapes),
+        out_shape=[
+            jax.ShapeDtypeStruct(shape, jnp.float32)
+            for shape in [(CHUNK, parts, rows, cols)] + carried_shapes
+        ],
         scratch_shapes=[pltpu.VMEM((GROUP, parts, width, cols), jnp.float32)],
         cost_estimate=pl.CostEstimate(
             flops=pairs * 500_000_000, bytes_accessed=pairs * 200_000, transcendentals=0
@@ -216,15 +231,17 @@
     slots = 4
     chunk, parts, _, columns = owns[0].shape
     shape = (chunk, parts, slots, 2, SUBLANES, columns)
-    block = pl.BlockSpec(shape[:3] + (1,) + shape[4:], lambda i: (0, 0, 0, half, 0, 0))
-    arrays = [a.reshape(shape) for a in (*owns, *received)]
+    size = shape[:3] + (1,) + shape[4:]
+    block = pl.BlockSpec(size, lambda i: (0, 0, 0, half, 0, 0))
+    alone = pl.BlockSpec(size, lambda i: (0,) * 6)
+    arrays = [a if a.shape == size else a.reshape(shape) for a in (*owns, *received)]
     out = jax.ShapeDtypeStruct((weight.shape[0] // 2, columns), jnp.float32)
     return pl.pallas_call(
         project_kernel,
         grid=(1,),
         in_specs=[
             pl.BlockSpec(memory_space=pltpu.SMEM), pl.BlockSpec(weight.shape, lambda i: (0, 0))
-        ] + [block] * len(arrays),
+        ] + [alone if a.shape == size else block for a in arrays],
         out_specs=[pl.BlockSpec(out.shape, lambda i: (0, 0))] * slots,
         out_shape=[out] * slots,
         cost_estimate=pl.CostEstimate(flops=400_000_000, bytes_accessed=2_000_000, transcendentals=0),
@@ -324,14 +341,16 @@
 
     owns, received = [], []
     for chunk, low in enumerate(lows):
-        own, carried = band_update(
+        own, *carried = band_update(
             chunk, own_cols, left, right, object_field, low, probe_modes, measured
         )
         owns.append(own)
-        received.append(shifted(carried, "strip", 1))
+        received.append([shifted(block, "strip", 1) for block in carried])
     mine = []
     for h in range(2):
-        share, *others = project(h, place, spread_solver, owns, received)
+        share, *others = project(
+            h, place, spread_solver, owns, [blocks[h % len(blocks)] for blocks in received]
+        )
         arrived = [along_x(other, d + 1) for d, other in enumerate(others)]
         share = share + arrived[0] + arrived[1] + arrived[2]
         arrived = along_z(share)
@@ -342,9 +361,7 @@
     refined = ()
     shape = (energies, parts, 4, 2, SUBLANES, columns)
     for h in range(2):
-        near = {d: along_x(mine[h], d) for d in (1, 3)}
-        far = along_x(near[1 + 2 * h], 1 + 2 * h)
-        pieces = [mine[h], near[1], far, near[3]]
+        pieces = [mine[h]] + [along_x(mine[h], d) for d in (1, 2, 3)]
         refined = (expand(h, place, spread_basis, pieces, shape, refined),)
     return refined[0].reshape(object_field.shape), abundance
 

time: 117 us -> 120 us (1.026)
  the two profiles are of different devices: /device:TPU:80 before, /device:TPU:87 now
where the time goes in v2:
time: 120 us
  starting transfers between devices  37.1 us (31%)
  waiting for transfers between devices  36.4 us (30%)
  Pallas kernels  29.1 us (24%)
  local copies, waits for them, and re-layouts  8.83 us (7%)
  other arithmetic  7.29 us (6%)
    ppermute x12, waiting for transfers between devices, along_x(): lax.ppermute(block, 'energy', [(e, (e + 2 * distance) % 8) for e in range...  23.3 us
    pallas_call x2, Pallas kernels, band_update(): pl.pallas_call(gradient_kernel, grid=(CHUNK // GROUP,), in_specs=[pl.Bloc...  17.1 us
    ppermute x5, starting transfers between devices, shifted(): return lax.ppermute(block, axis, route)  14.4 us
    ppermute x12, starting transfers between devices, along_x(): lax.ppermute(block, 'energy', [(e, (e + 2 * distance) % 8) for e in range...  13.8 us
    ppermute x2, starting transfers between devices, along_z(): return lax.ppermute(block, 'energy', [(e, e ^ 1) for e in range(8)])  8.96 us
    ppermute x2, waiting for transfers between devices, along_z(): return lax.ppermute(block, 'energy', [(e, e ^ 1) for e in range(8)])  8.52 us
    pallas_call x2, Pallas kernels, expand(): pl.pallas_call(expand_kernel, grid=(1,), in_specs=in_specs, out_specs=pl....  5.14 us
    pallas_call x2, Pallas kernels, project(): pl.pallas_call(project_kernel, grid=(1,), in_specs=[pl.BlockSpec(memory_s...  5.05 us
  transfers between devices with their start and end apart: 19, of which 9 were waited for; matrix products, arithmetic and copies ran while one was open for 9% of the time, Pallas kernels for 22%

profile of v2, /device:TPU:87, one launch (start us, length us, event | category | flops | bytes accessed | tf_op | source)
XLA Modules:
  0.0 120.0 jit_solution(2619241229671615882)
XLA Ops:
  0.7 2.4 %fusion.10 = (f32[4,2,64,384]{3,2,1,0:T(8,128)S(1)}, f32[4,2,64,384]{3,2,1,0:T(8,128)}) fusion(f32[8,2,64,384]{3,2,1,0:T(8,128)} %top_ref.3), kind=kLoop, calls=%fused_computation.35 | loop fusion | bytes 3145728 | tf_op jit(solution)/shard_map/slice | solution.py:329
  3.1 2.6 %collective-permute-start = (f32[4,2,64,384]{3,2,1,0:T(8,128)}, f32[4,2,64,384]{3,2,1,0:T(8,128)}, u32[]{:S(2)}, u32[]{:S(2)}) collective-permute-start(f32[4,2,64,384]{3,2,1,0:T(8,128)} %get-tuple-element.29), channel_id=1, source_target_pairs={{1,0},{2,1},{3,2},{4,3},{5,4},{6,5},{7,6},{8,7},{9,8},{10,9},{11,1... | collective-permute-start | bytes 2359304 | tf_op jit(solution)/shard_map/ppermute | solution.py:20
  5.6 1.9 %collective-permute-start.1 = (f32[4,2,64,384]{3,2,1,0:T(8,128)S(1)}, f32[4,2,64,384]{3,2,1,0:T(8,128)}, u32[]{:S(2)}, u32[]{:S(2)}) collective-permute-start(f32[4,2,64,384]{3,2,1,0:T(8,128)S(1)} %get-tuple-element.28), channel_id=1, source_target_pairs={{1,0},{2,1},{3,2},{4,3},{5,4},{6,5},{7,6},{8,7},{9,8},{10,9},{11,1... | collective-permute-start | bytes 2359304 | tf_op jit(solution)/shard_map/ppermute | solution.py:20
  14.4 2.7 %collective-permute-done.low_ref = f32[4,2,64,384]{3,2,1,0:T(8,128)} collective-permute-done((f32[4,2,64,384]{3,2,1,0:T(8,128)}, f32[4,2,64,384]{3,2,1,0:T(8,128)}, u32[]{:S(2)}, u32[]{:S(2)}) %collective-permute-start) | collective-permute-done | bytes 786464 | tf_op jit(solution)/shard_map/ppermute | solution.py:20
  17.1 8.5 %band_update.2 = (f32[4,2,64,384]{3,2,1,0:T(8,128)}, f32[4,2,64,384]{3,2,1,0:T(8,128)}) custom-call(s32[5]{0:T(128)} %dynamic-slice_reduce_fusion.cols_ref, bf16[256,256]{1,0:T(8,128)(2,1)} %constant.100.left_ref, bf16[256,256]{1,0:T(8,128)(2,1)} %constant.101.right_ref, f32[8,2,64,384]{3,2,1,0:T(8,128)} %top_ref.3, ...), custom_call_target="tpu_custom_call" | custom-call | flops 10000000000 | bytes 4000000 | tf_op jit(solution)/shard_map/band_update/pallas_call | solution.py:172
  25.7 1.9 %collective-permute-start.2 = (f32[4,2,64,384]{3,2,1,0:T(8,128)}, f32[4,2,64,384]{3,2,1,0:T(8,128)S(1)}, u32[]{:S(2)}, u32[]{:S(2)}) collective-permute-start(f32[4,2,64,384]{3,2,1,0:T(8,128)} %get-tuple-element.17), channel_id=1, source_target_pairs={{0,1},{1,2},{2,3},{3,4},{4,5},{5,6},{6,7},{7,8},{8,9},{9,10},{10,1... | collective-permute-start | bytes 2359304 | tf_op jit(solution)/shard_map/ppermute | solution.py:20
  27.6 8.6 %band_update.3 = (f32[4,2,64,384]{3,2,1,0:T(8,128)}, f32[4,2,4,1,8,384]{5,4,3,2,1,0:T(8,128)}, f32[4,2,4,1,8,384]{5,4,3,2,1,0:T(8,128)}) custom-call(s32[5]{0:T(128)} %dynamic-slice_reduce_fusion.cols_ref, bf16[256,256]{1,0:T(8,128)(2,1)} %constant.100.left_ref, bf16[256,256]{1,0:T(8,128)(2,1)} %constant.101.right_ref, f32[8,2,64,384]{3,2,1,0:T(8,128)} %top_ref.3, ...), custom_call_target="tpu_custom_call" | custom-call | flops 10000000000 | bytes 4000000 | tf_op jit(solution)/shard_map/band_update/pallas_call | solution.py:172
  36.2 6.1 %collective-permute-start.11 = (f32[4,2,4,1,8,384]{5,4,3,2,1,0:T(8,128)}, f32[4,2,4,1,8,384]{5,4,3,2,1,0:T(8,128)S(1)}, u32[]{:S(2)}, u32[]{:S(2)}) collective-permute-start(f32[4,2,4,1,8,384]{5,4,3,2,1,0:T(8,128)} %get-tuple-element.23), channel_id=1, source_target_pairs={{0,1},{1,2},{2,3},{3,4},{4,5},{5,6},{6,7},{7,8},{8,9},{9,10},{10,1... | collective-permute-start | bytes 1179656 | tf_op jit(solution)/shard_map/ppermute | solution.py:20
  42.3 1.9 %collective-permute-start.3 = (f32[4,2,4,1,8,384]{5,4,3,2,1,0:T(8,128)}, f32[4,2,4,1,8,384]{5,4,3,2,1,0:T(8,128)S(1)}, u32[]{:S(2)}, u32[]{:S(2)}) collective-permute-start(f32[4,2,4,1,8,384]{5,4,3,2,1,0:T(8,128)} %get-tuple-element.18), channel_id=1, source_target_pairs={{0,1},{1,2},{2,3},{3,4},{4,5},{5,6},{6,7},{7,8},{8,9},{9,10},{10,1... | collective-permute-start | bytes 1179656 | tf_op jit(solution)/shard_map/ppermute | solution.py:20
  48.4 2.5 %project.3 = (f32[128,384]{1,0:T(8,128)}, f32[128,384]{1,0:T(8,128)}, f32[128,384]{1,0:T(8,128)}, f32[128,384]{1,0:T(8,128)}) custom-call(s32[2]{0:T(128)} %pad_add_fusion.place_ref, bf16[256,256]{1,0:T(8,128)(2,1)} %maximum_maximum_fusion.1.weight_ref, f32[4,2,4,2,8,384]{5,4,3,2,1,0:T(8,128)} %bitcast.41, f32[4,2,4,2,8,384]{5,4,3,2,1,0:T(8,128)} %bitcast.45, ...), custom_call_target="tpu_custom_call" | custom-call | flops 400000000 | bytes 2000000 | tf_op jit(solution)/shard_map/project/pallas_call | solution.py:239
  54.8 2.5 %project.2 = (f32[128,384]{1,0:T(8,128)}, f32[128,384]{1,0:T(8,128)}, f32[128,384]{1,0:T(8,128)}, f32[128,384]{1,0:T(8,128)}) custom-call(s32[2]{0:T(128)} %pad_add_fusion.place_ref, bf16[256,256]{1,0:T(8,128)(2,1)} %maximum_maximum_fusion.1.weight_ref, f32[4,2,4,2,8,384]{5,4,3,2,1,0:T(8,128)} %bitcast.42, f32[4,2,4,2,8,384]{5,4,3,2,1,0:T(8,128)} %bitcast.46, ...), custom_call_target="tpu_custom_call" | custom-call | flops 400000000 | bytes 2000000 | tf_op jit(solution)/shard_map/project/pallas_call | solution.py:239
  57.4 1.8 %collective-permute-start.5 = (f32[128,384]{1,0:T(8,128)}, f32[128,384]{1,0:T(8,128)S(1)}, u32[]{:S(2)}, u32[]{:S(2)}) collective-permute-start(f32[128,384]{1,0:T(8,128)} %get-tuple-element.21), channel_id=1, source_target_pairs={{0,128},{32,160},{64,192},{96,224},{128,0},{160,32},{192,64},{224,... | collective-permute-start | bytes 589832 | tf_op jit(solution)/shard_map/ppermute | solution.py:315
  59.3 4.2 %collective-permute-done.14 = f32[128,384]{1,0:T(8,128)S(1)} collective-permute-done((f32[128,384]{1,0:T(8,128)}, f32[128,384]{1,0:T(8,128)S(1)}, u32[]{:S(2)}, u32[]{:S(2)}) %collective-permute-start.14) | collective-permute-done | bytes 196640 | tf_op jit(solution)/shard_map/ppermute | solution.py:315
  64.1 4.3 %collective-permute-start.15 = (f32[128,384]{1,0:T(8,128)S(1)}, f32[128,384]{1,0:T(8,128)S(1)}, u32[]{:S(2)}, u32[]{:S(2)}) collective-permute-start(f32[128,384]{1,0:T(8,128)S(1)} %add_add_fusion), channel_id=1, source_target_pairs={{0,32},{32,0},{64,96},{96,64},{128,160},{160,128},{192,224},{224,1... | collective-permute-start | bytes 589832 | tf_op jit(solution)/shard_map/ppermute | solution.py:319
  68.4 2.7 %collective-permute-done.6 = f32[128,384]{1,0:T(8,128)S(1)} collective-permute-done((f32[128,384]{1,0:T(8,128)}, f32[128,384]{1,0:T(8,128)S(1)}, u32[]{:S(2)}, u32[]{:S(2)}) %collective-permute-start.6) | collective-permute-done | bytes 196640 | tf_op jit(solution)/shard_map/ppermute | solution.py:315
  73.0 4.7 %collective-permute-start.7 = (f32[128,384]{1,0:T(8,128)S(1)}, f32[128,384]{1,0:T(8,128)S(1)}, u32[]{:S(2)}, u32[]{:S(2)}) collective-permute-start(f32[128,384]{1,0:T(8,128)S(1)} %add_add_fusion.1), channel_id=1, source_target_pairs={{0,32},{32,0},{64,96},{96,64},{128,160},{160,128},{192,224},{224,1... | collective-permute-start | bytes 589832 | tf_op jit(solution)/shard_map/ppermute | solution.py:319
  77.7 2.4 %collective-permute-start.16 = (f32[128,384]{1,0:T(8,128)S(1)}, f32[128,384]{1,0:T(8,128)S(1)}, u32[]{:S(2)}, u32[]{:S(2)}) collective-permute-start(f32[128,384]{1,0:T(8,128)S(1)} %add.62.refs_0_.first_ref), channel_id=1, source_target_pairs={{0,64},{32,96},{64,128},{96,160},{128,192},{160,224},{192,0},{224,... | collective-permute-start | bytes 589832 | tf_op jit(solution)/shard_map/ppermute | solution.py:315
  80.6 8.5 %collective-permute-done.7 = f32[128,384]{1,0:T(8,128)S(1)} collective-permute-done((f32[128,384]{1,0:T(8,128)S(1)}, f32[128,384]{1,0:T(8,128)S(1)}, u32[]{:S(2)}, u32[]{:S(2)}) %collective-permute-start.7) | collective-permute-done | bytes 196640 | tf_op jit(solution)/shard_map/ppermute | solution.py:319
  89.2 2.7 %collective-permute-start.8 = (f32[128,384]{1,0:T(8,128)S(1)}, f32[128,384]{1,0:T(8,128)S(1)}, u32[]{:S(2)}, u32[]{:S(2)}) collective-permute-start(f32[128,384]{1,0:T(8,128)S(1)} %add.58.refs_0_.second_ref), channel_id=1, source_target_pairs={{0,64},{32,96},{64,128},{96,160},{128,192},{160,224},{192,0},{224,... | collective-permute-start | bytes 589832 | tf_op jit(solution)/shard_map/ppermute | solution.py:315
  92.5 2.3 %collective-permute-start.17 = (f32[128,384]{1,0:T(8,128)S(1)}, f32[128,384]{1,0:T(8,128)S(1)}, u32[]{:S(2)}, u32[]{:S(2)}) collective-permute-start(f32[128,384]{1,0:T(8,128)S(1)} %add.62.refs_0_.first_ref), channel_id=1, source_target_pairs={{0,128},{32,160},{64,192},{96,224},{128,0},{160,32},{192,64},{224,... | collective-permute-start | bytes 589832 | tf_op jit(solution)/shard_map/ppermute | solution.py:315
  97.8 9.7 %collective-permute-done.17.refs_2_ = f32[128,384]{1,0:T(8,128)S(1)} collective-permute-done((f32[128,384]{1,0:T(8,128)S(1)}, f32[128,384]{1,0:T(8,128)S(1)}, u32[]{:S(2)}, u32[]{:S(2)}) %collective-permute-start.17) | collective-permute-done | bytes 196640 | tf_op jit(solution)/shard_map/ppermute | solution.py:315
  107.6 5.2 %collective-permute-done.18.refs_3_ = f32[128,384]{1,0:T(8,128)S(1)} collective-permute-done((f32[128,384]{1,0:T(8,128)S(1)}, f32[128,384]{1,0:T(8,128)S(1)}, u32[]{:S(2)}, u32[]{:S(2)}) %collective-permute-start.18) | collective-permute-done | bytes 196640 | tf_op jit(solution)/shard_map/ppermute | solution.py:315
  113.5 2.6 %expand.2.refs_4_ = f32[8,2,4,2,8,384]{5,4,3,2,1,0:T(8,128)} custom-call(s32[2]{0:T(128)} %pad_add_fusion.place_ref, bf16[256,256]{1,0:T(8,128)(2,1)} %maximum_maximum_fusion.weight_ref, f32[128,384]{1,0:T(8,128)} %copy-done.3, f32[128,384]{1,0:T(8,128)} %copy-done.10, f32[128,384]{1,0:T(8,128)} %copy-done.11, f32[128,384]{1,0:T(8,128)} %copy-done.12), custom_call_target="tpu_custom_call" | custom-call | flops 400000000 | bytes 2000000 | tf_op jit(solution)/shard_map/expand/pallas_call | solution.py:271
  117.5 2.6 %expand.3 = f32[8,2,4,2,8,384]{5,4,3,2,1,0:T(8,128)} custom-call(s32[2]{0:T(128)} %pad_add_fusion.place_ref, bf16[256,256]{1,0:T(8,128)(2,1)} %maximum_maximum_fusion.weight_ref, f32[128,384]{1,0:T(8,128)} %copy-done.2, f32[128,384]{1,0:T(8,128)} %copy-done.6, f32[128,384]{1,0:T(8,128)} %copy-done.7, ...), custom_call_target="tpu_custom_call", output_to_operand_aliasing={{}: (6, {})} | custom-call | flops 400000000 | bytes 2000000 | tf_op jit(solution)/shard_map/expand/pallas_call | solution.py:271
  (82 shorter events, 23.8 us)
Async XLA Ops:
  0.6 13.0 %copy-start = (s32[32,5]{0,1:T(8,128)S(1)}, s32[32,5]{0,1:T(8,128)}, u32[]{:S(2)}) copy-start(s32[32,5]{0,1:T(8,128)} %param.11) | copy-start | bytes 1924
  3.1 14.1 %collective-permute-start = (f32[4,2,64,384]{3,2,1,0:T(8,128)}, f32[4,2,64,384]{3,2,1,0:T(8,128)}, u32[]{:S(2)}, u32[]{:S(2)}) collective-permute-start(f32[4,2,64,384]{3,2,1,0:T(8,128)} %get-tuple-element.29), channel_id=1, source_target_pairs={{1,0},{2,1},{3,2},{4,3},{5,4},{6,5},{7,6},{8,7},{9,8},{10,9},{11,1... | collective-permute-start | bytes 2359304 | tf_op jit(solution)/shard_map/ppermute | solution.py:20
  5.6 21.9 %collective-permute-start.1 = (f32[4,2,64,384]{3,2,1,0:T(8,128)S(1)}, f32[4,2,64,384]{3,2,1,0:T(8,128)}, u32[]{:S(2)}, u32[]{:S(2)}) collective-permute-start(f32[4,2,64,384]{3,2,1,0:T(8,128)S(1)} %get-tuple-element.28), channel_id=1, source_target_pairs={{1,0},{2,1},{3,2},{4,3},{5,4},{6,5},{7,6},{8,7},{9,8},{10,9},{11,1... | collective-permute-start | bytes 2359304 | tf_op jit(solution)/shard_map/ppermute | solution.py:20
  25.7 21.6 %collective-permute-start.2 = (f32[4,2,64,384]{3,2,1,0:T(8,128)}, f32[4,2,64,384]{3,2,1,0:T(8,128)S(1)}, u32[]{:S(2)}, u32[]{:S(2)}) collective-permute-start(f32[4,2,64,384]{3,2,1,0:T(8,128)} %get-tuple-element.17), channel_id=1, source_target_pairs={{0,1},{1,2},{2,3},{3,4},{4,5},{5,6},{6,7},{7,8},{8,9},{9,10},{10,1... | collective-permute-start | bytes 2359304 | tf_op jit(solution)/shard_map/ppermute | solution.py:20
  36.2 11.1 %collective-permute-start.11 = (f32[4,2,4,1,8,384]{5,4,3,2,1,0:T(8,128)}, f32[4,2,4,1,8,384]{5,4,3,2,1,0:T(8,128)S(1)}, u32[]{:S(2)}, u32[]{:S(2)}) collective-permute-start(f32[4,2,4,1,8,384]{5,4,3,2,1,0:T(8,128)} %get-tuple-element.23), channel_id=1, source_target_pairs={{0,1},{1,2},{2,3},{3,4},{4,5},{5,6},{6,7},{7,8},{8,9},{9,10},{10,1... | collective-permute-start | bytes 1179656 | tf_op jit(solution)/shard_map/ppermute | solution.py:20
  42.3 11.8 %collective-permute-start.3 = (f32[4,2,4,1,8,384]{5,4,3,2,1,0:T(8,128)}, f32[4,2,4,1,8,384]{5,4,3,2,1,0:T(8,128)S(1)}, u32[]{:S(2)}, u32[]{:S(2)}) collective-permute-start(f32[4,2,4,1,8,384]{5,4,3,2,1,0:T(8,128)} %get-tuple-element.18), channel_id=1, source_target_pairs={{0,1},{1,2},{2,3},{3,4},{4,5},{5,6},{6,7},{7,8},{8,9},{9,10},{10,1... | collective-permute-start | bytes 1179656 | tf_op jit(solution)/shard_map/ppermute | solution.py:20
  50.9 13.2 %copy-start.9 = (f32[128,384]{1,0:T(8,128)S(1)}, f32[128,384]{1,0:T(8,128)}, u32[]{:S(2)}) copy-start(f32[128,384]{1,0:T(8,128)} %get-tuple-element.24) | copy-start | bytes 589828
  50.9 12.6 %collective-permute-start.14 = (f32[128,384]{1,0:T(8,128)}, f32[128,384]{1,0:T(8,128)S(1)}, u32[]{:S(2)}, u32[]{:S(2)}) collective-permute-start(f32[128,384]{1,0:T(8,128)} %get-tuple-element.27), channel_id=1, source_target_pairs={{0,192},{32,224},{64,0},{96,32},{128,64},{160,96},{192,128},{224,1... | collective-permute-start | bytes 589832 | tf_op jit(solution)/shard_map/ppermute | solution.py:315
  51.4 12.0 %collective-permute-start.13 = (f32[128,384]{1,0:T(8,128)}, f32[128,384]{1,0:T(8,128)S(1)}, u32[]{:S(2)}, u32[]{:S(2)}) collective-permute-start(f32[128,384]{1,0:T(8,128)} %get-tuple-element.26), channel_id=1, source_target_pairs={{0,128},{32,160},{64,192},{96,224},{128,0},{160,32},{192,64},{224,... | collective-permute-start | bytes 589832 | tf_op jit(solution)/shard_map/ppermute | solution.py:315
  52.3 11.8 %collective-permute-start.12 = (f32[128,384]{1,0:T(8,128)}, f32[128,384]{1,0:T(8,128)S(1)}, u32[]{:S(2)}, u32[]{:S(2)}) collective-permute-start(f32[128,384]{1,0:T(8,128)} %get-tuple-element.25), channel_id=1, source_target_pairs={{0,64},{32,96},{64,128},{96,160},{128,192},{160,224},{192,0},{224,... | collective-permute-start | bytes 589832 | tf_op jit(solution)/shard_map/ppermute | solution.py:315
  57.4 13.7 %collective-permute-start.6 = (f32[128,384]{1,0:T(8,128)}, f32[128,384]{1,0:T(8,128)S(1)}, u32[]{:S(2)}, u32[]{:S(2)}) collective-permute-start(f32[128,384]{1,0:T(8,128)} %get-tuple-element.22), channel_id=1, source_target_pairs={{0,192},{32,224},{64,0},{96,32},{128,64},{160,96},{192,128},{224,1... | collective-permute-start | bytes 589832 | tf_op jit(solution)/shard_map/ppermute | solution.py:315
  57.4 13.6 %collective-permute-start.5 = (f32[128,384]{1,0:T(8,128)}, f32[128,384]{1,0:T(8,128)S(1)}, u32[]{:S(2)}, u32[]{:S(2)}) collective-permute-start(f32[128,384]{1,0:T(8,128)} %get-tuple-element.21), channel_id=1, source_target_pairs={{0,128},{32,160},{64,192},{96,224},{128,0},{160,32},{192,64},{224,... | collective-permute-start | bytes 589832 | tf_op jit(solution)/shard_map/ppermute | solution.py:315
  63.4 8.6 %collective-permute-start.4 = (f32[128,384]{1,0:T(8,128)}, f32[128,384]{1,0:T(8,128)S(1)}, u32[]{:S(2)}, u32[]{:S(2)}) collective-permute-start(f32[128,384]{1,0:T(8,128)} %get-tuple-element.20), channel_id=1, source_target_pairs={{0,64},{32,96},{64,128},{96,160},{128,192},{160,224},{192,0},{224,... | collective-permute-start | bytes 589832 | tf_op jit(solution)/shard_map/ppermute | solution.py:315
  64.1 13.5 %collective-permute-start.15 = (f32[128,384]{1,0:T(8,128)S(1)}, f32[128,384]{1,0:T(8,128)S(1)}, u32[]{:S(2)}, u32[]{:S(2)}) collective-permute-start(f32[128,384]{1,0:T(8,128)S(1)} %add_add_fusion), channel_id=1, source_target_pairs={{0,32},{32,0},{64,96},{96,64},{128,160},{160,128},{192,224},{224,1... | collective-permute-start | bytes 589832 | tf_op jit(solution)/shard_map/ppermute | solution.py:319
  73.0 16.1 %collective-permute-start.7 = (f32[128,384]{1,0:T(8,128)S(1)}, f32[128,384]{1,0:T(8,128)S(1)}, u32[]{:S(2)}, u32[]{:S(2)}) collective-permute-start(f32[128,384]{1,0:T(8,128)S(1)} %add_add_fusion.1), channel_id=1, source_target_pairs={{0,32},{32,0},{64,96},{96,64},{128,160},{160,128},{192,224},{224,1... | collective-permute-start | bytes 589832 | tf_op jit(solution)/shard_map/ppermute | solution.py:319
  77.7 18.4 %copy-start.3 = (f32[128,384]{1,0:T(8,128)}, f32[128,384]{1,0:T(8,128)S(1)}, u32[]{:S(2)}) copy-start(f32[128,384]{1,0:T(8,128)S(1)} %add.62.refs_0_.first_ref) | copy-start | bytes 589828
  77.7 17.1 %collective-permute-start.16 = (f32[128,384]{1,0:T(8,128)S(1)}, f32[128,384]{1,0:T(8,128)S(1)}, u32[]{:S(2)}, u32[]{:S(2)}) collective-permute-start(f32[128,384]{1,0:T(8,128)S(1)} %add.62.refs_0_.first_ref), channel_id=1, source_target_pairs={{0,64},{32,96},{64,128},{96,160},{128,192},{160,224},{192,0},{224,... | collective-permute-start | bytes 589832 | tf_op jit(solution)/shard_map/ppermute | solution.py:315
  89.2 7.0 %copy-start.2 = (f32[128,384]{1,0:T(8,128)}, f32[128,384]{1,0:T(8,128)S(1)}, u32[]{:S(2)}) copy-start(f32[128,384]{1,0:T(8,128)S(1)} %add.58.refs_0_.second_ref) | copy-start | bytes 589828
  89.2 26.9 %collective-permute-start.8 = (f32[128,384]{1,0:T(8,128)S(1)}, f32[128,384]{1,0:T(8,128)S(1)}, u32[]{:S(2)}, u32[]{:S(2)}) collective-permute-start(f32[128,384]{1,0:T(8,128)S(1)} %add.58.refs_0_.second_ref), channel_id=1, source_target_pairs={{0,64},{32,96},{64,128},{96,160},{128,192},{160,224},{192,0},{224,... | collective-permute-start | bytes 589832 | tf_op jit(solution)/shard_map/ppermute | solution.py:315
  91.8 24.2 %collective-permute-start.9 = (f32[128,384]{1,0:T(8,128)S(1)}, f32[128,384]{1,0:T(8,128)S(1)}, u32[]{:S(2)}, u32[]{:S(2)}) collective-permute-start(f32[128,384]{1,0:T(8,128)S(1)} %add.58.refs_0_.second_ref), channel_id=1, source_target_pairs={{0,128},{32,160},{64,192},{96,224},{128,0},{160,32},{192,64},{224,... | collective-permute-start | bytes 589832 | tf_op jit(solution)/shard_map/ppermute | solution.py:315
  92.2 23.9 %collective-permute-start.10 = (f32[128,384]{1,0:T(8,128)S(1)}, f32[128,384]{1,0:T(8,128)S(1)}, u32[]{:S(2)}, u32[]{:S(2)}) collective-permute-start(f32[128,384]{1,0:T(8,128)S(1)} %add.58.refs_0_.second_ref), channel_id=1, source_target_pairs={{0,192},{32,224},{64,0},{96,32},{128,64},{160,96},{192,128},{224,1... | collective-permute-start | bytes 589832 | tf_op jit(solution)/shard_map/ppermute | solution.py:315
  92.5 15.1 %collective-permute-start.17 = (f32[128,384]{1,0:T(8,128)S(1)}, f32[128,384]{1,0:T(8,128)S(1)}, u32[]{:S(2)}, u32[]{:S(2)}) collective-permute-start(f32[128,384]{1,0:T(8,128)S(1)} %add.62.refs_0_.first_ref), channel_id=1, source_target_pairs={{0,128},{32,160},{64,192},{96,224},{128,0},{160,32},{192,64},{224,... | collective-permute-start | bytes 589832 | tf_op jit(solution)/shard_map/ppermute | solution.py:315
  94.8 18.0 %copy-start.10 = (f32[128,384]{1,0:T(8,128)}, f32[128,384]{1,0:T(8,128)S(1)}, u32[]{:S(2)}) copy-start(f32[128,384]{1,0:T(8,128)S(1)} %collective-permute-done.16.refs_1_) | copy-start | bytes 589828
  94.8 18.0 %collective-permute-start.18 = (f32[128,384]{1,0:T(8,128)S(1)}, f32[128,384]{1,0:T(8,128)S(1)}, u32[]{:S(2)}, u32[]{:S(2)}) collective-permute-start(f32[128,384]{1,0:T(8,128)S(1)} %add.62.refs_0_.first_ref), channel_id=1, source_target_pairs={{0,192},{32,224},{64,0},{96,32},{128,64},{160,96},{192,128},{224,1... | collective-permute-start | bytes 589832 | tf_op jit(solution)/shard_map/ppermute | solution.py:315
  (9 other events, 17.5 us)
